TPU v7x, 128 devices: a whole 4x4x4 slice. The times are simulated.
128 devices in a mesh: dap: 4 (over z_lo, core), dp: 32 (over z_hi, y, x).
Axes of the slice: x: 4, y: 4, z: 4 (z_hi: 2, z_lo: 2; z = z_hi * 2 + z_lo), core: 2. Of those that a mesh axis runs over, the one named last changes fastest.
Arguments:
- pair_rep: bfloat16 [32, 128, 128, 128], P('dp', 'dap'), may hold values from -6 to 6
- cotangent: bfloat16 [32, 128, 128, 128], P('dp', 'dap'), may hold values from -6 to 6
- tok_mask: int32 [32, 128], P('dp'), may hold values from 0 to 1, as said below
- tok_types: int32 [32, 128], P('dp'), may hold values from 0 to 3
- pair_mask: int32 [32, 128, 128], P('dp', 'dap'), may hold values 0 or 1
- triangle_gain: float32 [128], replicated, may hold values from 0.5 to 1.5
- triangle_input: bfloat16 [128, 512], replicated, may hold values from -0.5 to 0.5
- triangle_gating: bfloat16 [128, 128], replicated, may hold values from -0.5 to 0.5
- product_gain: float32 [128], replicated, may hold values from 0.5 to 1.5
- triangle_output: bfloat16 [128, 128], replicated, may hold values from -0.5 to 0.5
- attend_gain: float32 [128], replicated, may hold values from 0.5 to 1.5
- attend_bias: bfloat16 [128, 4], replicated, may hold values from -0.5 to 0.5
- attend_input: bfloat16 [128, 512], replicated, may hold values from -0.5 to 0.5
- attend_output: bfloat16 [128, 128], replicated, may hold values from -0.5 to 0.5
- type_table: float32 [4, 4, 4], replicated, may hold values from -4 to 4
Outputs:
- pair_out: bfloat16 [32, 128, 128, 128], P('dp', 'dap')
- pair_grad: bfloat16 [32, 128, 128, 128], P('dp', 'dap')
- grad_triangle_gain: float32 [128], replicated
- grad_triangle_input: float32 [128, 512], replicated
- grad_triangle_gating: float32 [128, 128], replicated
- grad_product_gain: float32 [128], replicated
- grad_triangle_output: float32 [128, 128], replicated
- grad_attend_gain: float32 [128], replicated
- grad_attend_bias: float32 [128, 4], replicated
- grad_attend_input: float32 [128, 512], replicated
- grad_attend_output: float32 [128, 128], replicated
- grad_type_table: float32 [4, 4, 4], replicated
Inputs may be any that keep to these rules, and one draw needn't show every extreme that they name: `tok_mask`: each crop's real tokens form a leading run of at least 64 tokens.
All inputs are finite; a program needn't handle non-finite values. No bound on the sum of `pair_mask` on one device may be relied on, other than what follows from the above.
Results may differ from a plain program's by a relative error of at most 0.035.
Values may be sent and summed in bfloat16 or wider, within the bound.
A program may use at most 128 MiB of HBM per device.

v0:
```python
from functools import partial

import jax
import jax.numpy as jnp
from jax import lax
from jax.sharding import PartitionSpec as P

EPSILON = 1e-05


def layer_norm(values, scales):
    centred = values - jnp.mean(values, axis=-1, keepdims=True)
    spread = jnp.mean(centred * centred, axis=-1, keepdims=True)
    return centred * lax.rsqrt(spread + EPSILON) * scales


def triangle_first(slab, scales, input_w, gating_w, pair_live):
    channels = slab.shape[-1]
    normed = layer_norm(slab.astype(jnp.float32), scales).astype(jnp.bfloat16)
    projected = jnp.einsum("ijc,cd->ijd", normed, input_w, preferred_element_type=jnp.float32)
    masked = pair_live[..., None]
    left_proj = (
        jax.nn.sigmoid(projected[..., channels : 2 * channels]) * projected[..., :channels] * masked
    ).astype(jnp.bfloat16)
    right_proj = (
        jax.nn.sigmoid(projected[..., 3 * channels :])
        * projected[..., 2 * channels : 3 * channels]
        * masked
    ).astype(jnp.bfloat16)
    out_gate = jax.nn.sigmoid(
        jnp.einsum("ijc,cd->ijd", normed, gating_w, preferred_element_type=jnp.float32)
    )
    return (left_proj, right_proj, out_gate)


def triangle_second(slab, product, out_gate, scales, output_w):
    normed = layer_norm(product, scales).astype(jnp.bfloat16)
    update = out_gate * jnp.einsum(
        "ijc,cd->ijd", normed, output_w, preferred_element_type=jnp.float32
    )
    return (slab.astype(jnp.float32) + update).astype(jnp.bfloat16)


def attend_first(middle, scales, bias_w):
    normed = layer_norm(middle.astype(jnp.float32), scales).astype(jnp.bfloat16)
    bias_rows = jnp.einsum(
        "rjc,ch->hrj", normed, bias_w, preferred_element_type=jnp.float32
    ).astype(jnp.bfloat16)
    return (normed, bias_rows)


def attend_second(middle, normed, bias_all, table, input_w, output_w, one_hot, key_live):
    row_count, length, channels = middle.shape
    head_count = bias_all.shape[0]
    head_size = channels // head_count
    projected = jnp.einsum("ijc,cd->ijd", normed, input_w, preferred_element_type=jnp.float32)
    query = (
        projected[..., :channels]
        .astype(jnp.bfloat16)
        .reshape(row_count, length, head_count, head_size)
    )
    keys_all = (
        projected[..., channels : 2 * channels]
        .astype(jnp.bfloat16)
        .reshape(row_count, length, head_count, head_size)
    )
    values_all = (
        projected[..., 2 * channels : 3 * channels]
        .astype(jnp.bfloat16)
        .reshape(row_count, length, head_count, head_size)
    )
    gate = jax.nn.sigmoid(projected[..., 3 * channels :])
    type_bias = jnp.einsum("ja,hab,kb->hjk", one_hot, table, one_hot)
    scores = jnp.einsum(
        "rjhd,rkhd->rhjk", query, keys_all, preferred_element_type=jnp.float32
    ) / jnp.sqrt(jnp.float32(head_size))
    scores = scores + (bias_all + type_bias)[None]
    exponent = jnp.exp(scores) * key_live[:, None, None, :]
    totals = jnp.maximum(jnp.sum(exponent, axis=-1, keepdims=True), 1.0)
    weights = (exponent / totals).astype(jnp.bfloat16)
    attended = jnp.einsum(
        "rhjk,rkhd->rjhd", weights, values_all, preferred_element_type=jnp.float32
    ).reshape(row_count, length, channels)
    gated = (gate * attended).astype(jnp.bfloat16)
    update = jnp.einsum("ijc,cd->ijd", gated, output_w, preferred_element_type=jnp.float32)
    return (middle.astype(jnp.float32) + update).astype(jnp.bfloat16)


def per_device(
    pair_rep,
    cotangent,
    tok_mask,
    tok_types,
    pair_mask,
    triangle_gain,
    triangle_input,
    triangle_gating,
    product_gain,
    triangle_output,
    attend_gain,
    attend_bias,
    attend_input,
    attend_output,
    type_table,
):
    slab = pair_rep[0]
    row_count = slab.shape[0]
    length = slab.shape[1]
    tokens = tok_mask[0].astype(jnp.float32)
    first_row = lax.axis_index("dap") * row_count
    row_tokens = lax.dynamic_slice_in_dim(tokens, first_row, row_count)
    pair_live = pair_mask[0].astype(jnp.float32) * row_tokens[:, None] * tokens[None, :]
    one_hot = (
        tok_types[0][:, None] == jnp.arange(type_table.shape[1], dtype=jnp.int32)[None, :]
    ).astype(jnp.float32)
    first_out, first_back = jax.vjp(
        partial(triangle_first, pair_live=pair_live),
        slab,
        triangle_gain,
        triangle_input,
        triangle_gating,
    )
    left_proj, right_proj, out_gate = first_out
    right_all = lax.all_gather(right_proj, "dap", axis=0, tiled=True)
    product = jnp.einsum("ikc,jkc->ijc", left_proj, right_all, preferred_element_type=jnp.float32)
    middle, second_back = jax.vjp(
        triangle_second, slab, product, out_gate, product_gain, triangle_output
    )
    third_out, third_back = jax.vjp(attend_first, middle, attend_gain, attend_bias)
    normed, bias_rows = third_out
    bias_all = lax.all_gather(bias_rows, "dap", axis=1, tiled=True).astype(jnp.float32)
    pair_out, fourth_back = jax.vjp(
        partial(attend_second, one_hot=one_hot, key_live=pair_live),
        middle,
        normed,
        bias_all,
        type_table,
        attend_input,
        attend_output,
    )
    d_middle_a, d_normed, d_bias_all, d_table, d_att_in, d_att_out = fourth_back(cotangent[0])
    d_bias_rows = lax.psum_scatter(
        d_bias_all.astype(jnp.bfloat16), "dap", scatter_dimension=1, tiled=True
    )
    d_middle_b, d_att_gain, d_att_bias = third_back((d_normed, d_bias_rows))
    attend_terms = (
        d_att_gain,
        d_att_bias.astype(jnp.float32),
        d_att_in.astype(jnp.float32),
        d_att_out.astype(jnp.float32),
        d_table,
    )
    d_middle = d_middle_a + d_middle_b
    d_slab_c, d_product, d_gate, d_prod_gain, d_tri_out = second_back(d_middle)
    d_left = jnp.einsum(
        "ijc,jkc->ikc", d_product, right_all, preferred_element_type=jnp.float32
    ).astype(jnp.bfloat16)
    d_right = lax.psum_scatter(
        jnp.einsum("ijc,ikc->jkc", d_product, left_proj, preferred_element_type=jnp.float32).astype(
            jnp.bfloat16
        ),
        "dap",
        scatter_dimension=0,
        tiled=True,
    ).astype(jnp.float32)
    d_right = d_right.astype(jnp.bfloat16)
    d_slab_d, d_tri_gain, d_tri_in, d_tri_gate = first_back((d_left, d_right, d_gate))
    d_slab = d_slab_c + d_slab_d
    triangle_terms = (
        d_tri_gain,
        d_tri_in.astype(jnp.float32),
        d_tri_gate.astype(jnp.float32),
        d_prod_gain,
        d_tri_out.astype(jnp.float32),
    )
    summed_all = lax.psum(triangle_terms + attend_terms, ("dap", "dp"))
    triangle_summed = summed_all[:5]
    attend_summed = summed_all[5:]
    factor = (length * length * lax.axis_size("dp")) ** (-0.5)
    return (
        pair_out[None],
        d_slab[None],
        triangle_summed[0] * factor,
        triangle_summed[1] * factor,
        triangle_summed[2] * factor,
        triangle_summed[3] * factor,
        triangle_summed[4] * factor,
        attend_summed[0] * factor,
        attend_summed[1] * factor,
        attend_summed[2] * factor,
        attend_summed[3] * factor,
        attend_summed[4] * factor,
    )


def solution(mesh):
    return jax.shard_map(
        per_device,
        mesh=mesh,
        in_specs=(
            P("dp", "dap", None, None),
            P("dp", "dap", None, None),
            P("dp", None),
            P("dp", None),
            P("dp", "dap", None),
            P(),
            P(),
            P(),
            P(),
            P(),
            P(),
            P(),
            P(),
            P(),
            P(),
        ),
        out_specs=(
            P("dp", "dap", None, None),
            P("dp", "dap", None, None),
            P(),
            P(),
            P(),
            P(),
            P(),
            P(),
            P(),
            P(),
            P(),
            P(),
        ),
        check_vma=False,
    )
```

profile of v0, /device:TPU:1, one launch (start us, length us, event | category | flops | bytes accessed | tf_op | source)
XLA Modules:
  0.0 484.0 jit_solution(14713057218166650713)
XLA Ops:
  7.3 1.7 copy.124
  11.1 2.7 multiply_convert_fusion.1
  18.8 47.5 %all-gather.2.cloned.1.call-done = bf16[128,128,128]{2,1,0:T(8,128)(2,1)} async-done(((bf16[32,128,128]{2,1,0:T(8,128)(2,1)}), bf16[128,128,128]{2,1,0:T(8,128)(2,1)}) %all-gather.2.cloned.1.call-update) | async-done | bytes 4194320 | tf_op jit(solution)/shard_map/all_gather | solution.py:124
  66.3 6.7 %copy.133 = bf16[128,128,128]{1,0,2:T(8,128)(2,1)} copy(bf16[128,128,128]{2,1,0:T(8,128)(2,1)} %all-gather.2.cloned.1.call-done) | data formatting | bytes 8388608 | tf_op jit(solution)/shard_map/all_gather | solution.py:124
  73.1 4.8 bitcast_reduce_fusion
  79.7 2.5 convert_reduce_fusion
  82.6 3.3 fusion.166
  86.0 1.6 slice.39
  87.6 2.9 copy.206
  90.5 3.7 fusion.164
  94.2 2.3 copy.139
  96.5 1.7 fusion.93
  98.1 5.3 %all_gather.7 = bf16[4,128,128]{2,0,1:T(4,128)(2,1)S(1)} all-gather(bf16[4,32,128]{2,0,1:T(4,128)(2,1)S(1)} %fusion.93), channel_id=1, replica_groups=mesh['dap'=4,'dp'=32] {'dap'}, dimensions={1}, use_global_device_ids=true | all-gather | bytes 163840 | tf_op jit(solution)/shard_map/all_gather | solution.py:131
  105.5 2.4 copy.140
  107.9 2.3 copy.141
  110.1 4.3 multiply_reduce_fusion
  114.5 1.6 convert_multiply_fusion.9
  116.1 4.5 fusion.4
  120.7 5.5 %fusion.161 = (bf16[4,128,128]{1,2,0:T(8,128)(2,1)S(1)}, f32[32,4,128,128]{2,3,1,0:T(8,128)S(1)}, bf16[32,4,128,128]{2,3,1,0:T(8,128)(2,1)S(1)}) fusion(f32[4,128,128]{1,2,0:T(8,128)} %copy-done.27, f32[32,4,128,128]{2,3,1,0:T(8,128)S(1)} %get-tuple-element.96, f32[32,128]{1,0:T(8,128)S(1)} %copy-done.44, f32[32,4,128]{2,1,0:T(4,128)S(1)} %get-tuple-element.84, ...), kind=kLoop, calls=%fused_computation.231 | loop fusion | flops 23003136 | bytes 25706496 | tf_op jit(solution)/shard_map/transpose(jvp())/reduce_sum | solution.py:77
  126.2 3.5 fusion.70
  129.8 3.3 fusion.67
  133.1 2.5 fusion.167
  135.6 3.3 fusion.168
  140.0 4.6 fusion.41
  144.6 1.4 copy-done.25
  146.0 1.7 fusion.65
  147.7 28.9 %all-reduce.14.cloned.1.call-done = bf16[4,128,128]{2,0,1:T(4,128)(2,1)} async-done(((bf16[4,128,128]{2,0,1:T(4,128)(2,1)}), bf16[4,128,128]{2,0,1:T(4,128)(2,1)}) %all-reduce.14.cloned.1.call-update) | async-done | bytes 131088
  176.7 2.5 fusion.47
  179.2 2.0 fusion.42
  183.6 1.9 fusion.44
  187.9 3.3 fusion.63
  191.2 6.8 %copy.160 = bf16[128,128,128]{1,0,2:T(8,128)(2,1)} copy(bf16[128,128,128]{2,1,0:T(8,128)(2,1)} %fusion.63) | data formatting | bytes 8388608 | tf_op jit(solution)/shard_map/ijc,ikc->jkc/dot_general | solution.py:159
  199.6 1.5 fusion.77
  201.0 2.3 copy.172
  203.6 2.4 fusion.90
  206.0 3.9 fusion.85
  209.9 1.4 fusion.95
  213.1 1.5 fusion.88
  217.3 27.1 %reduce-scatter.2.cloned.1.call-done = bf16[32,128,128]{1,2,0:T(8,128)(2,1)} async-done(((bf16[128,128,128]{1,2,0:T(8,128)(2,1)}), bf16[32,128,128]{1,2,0:T(8,128)(2,1)}) %reduce-scatter.2.cloned.1.call-update) | async-done | bytes 1048592 | tf_op jit(solution)/shard_map/reduce_scatter | solution.py:158
  244.4 5.1 %fusion.60 = (f32[32,128,128]{1,2,0:T(8,128)S(1)}, f32[32,128,128]{1,2,0:T(8,128)S(1)}, f32[32,128,128]{1,2,0:T(8,128)S(1)}, f32[32,128,128]{1,2,0:T(8,128)S(1)}) fusion(bf16[32,128,128]{1,2,0:T(8,128)(2,1)} %reduce-scatter.2.cloned.1.call-done, f32[32,128]{1,0:T(8,128)S(1)} %copy-done.45, f32[32,128,512]{1,2,0:T(8,128)} %copy-done.2, ...), kind=kLoop, calls=%fused_computation.101 | loop fusion | flops 10485760 | bytes 18890752 | tf_op jit(solution)/shard_map/transpose(jvp())/mul | solution.py:26
  250.5 2.2 fusion.83
  252.7 3.3 fusion.39
  256.0 1.5 fusion.45
  260.0 65.8 %all-reduce.9 = (f32[128]{0:T(128)S(1)}, f32[128]{0:T(128)S(1)}, f32[128]{0:T(128)S(1)}, f32[128,4]{0,1:T(4,128)S(1)}, f32[4,4,4]{1,2,0:T(4,128)S(1)}) all-reduce(f32[128]{0:T(128)S(1)} %get-tuple-element.52, f32[128]{0:T(128)S(1)} %get-tuple-element.48, f32[128]{0:T(128)S(1)} %copy-done.70, ...), channel_id=1, replica_groups=mesh['dap'=4,'dp'=32] {'dap','dp'}, use_global_device_ids=true, to_apply=%region_18.0 | all-reduce | flops 960 | bytes 7680 | tf_op jit(solution)/shard_map/psum | solution.py:176
  328.1 144.0 %all-reduce.16.cloned.1.call-done = (f32[128,512]{1,0:T(8,128)}, f32[128,128]{1,0:T(8,128)}, f32[128,128]{1,0:T(8,128)}, f32[128,512]{1,0:T(8,128)}, f32[128,128]{1,0:T(8,128)}) async-done(((f32[128,512]{1,0:T(8,128)}, f32[128,128]{1,0:T(8,128)}, f32[128,128]{1,0:T(8,128)}, f32[128,512]{1,0:T(8,128)}, f32[128,128]{1,0:T(8,128)}), (f32[128,512]{1,0:T(8,128)}, f32[128,128]{1,0:T(8,128)}, ...) | async-done | bytes 720912 | tf_op jit(solution)/shard_map/psum | solution.py:176
  472.1 1.5 broadcast_multiply_fusion.4
  473.6 1.9 broadcast_multiply_fusion
  475.5 1.5 broadcast_multiply_fusion.2
  (203 shorter events, 28.5 us)
Async XLA Ops:
  7.2 75.4 %copy-start = (bf16[128,512]{1,0:T(8,128)(2,1)S(1)}, bf16[128,512]{1,0:T(8,128)(2,1)}, u32[]{:S(2)}) copy-start(bf16[128,512]{1,0:T(8,128)(2,1)} %param.27) | copy-start | bytes 393220
  7.2 59.2 %all-gather.2.cloned.1.call-start = ((), (), s32[]{:S(2)}) async-start(), calls=%async_computation.1 | async-start | bytes 5242880 | tf_op jit(solution)/shard_map/all_gather | solution.py:124
  7.2 2.3 copy-start.73
  7.3 2.4 copy-start.52
  7.3 2.4 copy-start.61
  9.6 69.8 %copy-start.33 = (f32[32,128]{1,0:T(8,128)}, f32[32,128]{1,0:T(8,128)S(1)}, u32[]{:S(2)}) copy-start(f32[32,128]{1,0:T(8,128)S(1)} %fusion.126) | copy-start | bytes 49156
  11.0 3.6 copy-start.2
  11.1 3.5 copy-start.43
  15.9 2.8 copy-start.63
  16.0 160.7 %all-reduce.14.cloned.1.call-start = ((), (), s32[]{:S(2)}) async-start(), calls=%async_computation.3 | async-start | bytes 262144
  78.9 3.3 copy-start.16
  79.7 2.5 copy-start.13
  79.7 3.0 copy-start.68
  82.2 3.8 copy-start.8
  82.2 14.2 %copy-start.35 = (f32[32,128]{1,0:T(8,128)}, f32[32,128]{1,0:T(8,128)S(1)}, u32[]{:S(2)}) copy-start(f32[32,128]{1,0:T(8,128)S(1)} %broadcast_multiply_fusion.5) | copy-start | bytes 49156
  82.6 3.4 copy-start.50
  82.6 13.8 %copy-start.39 = (f32[32,128]{1,0:T(8,128)}, f32[32,128]{1,0:T(8,128)S(1)}, u32[]{:S(2)}) copy-start(f32[32,128]{1,0:T(8,128)S(1)} %fusion.128) | copy-start | bytes 49156
  94.2 2.3 copy-start.71
  105.5 10.6 %copy-start.27 = (f32[4,128,128]{1,2,0:T(8,128)}, f32[4,128,128]{1,2,0:T(8,128)S(1)}, u32[]{:S(2)}) copy-start(f32[4,128,128]{1,2,0:T(8,128)S(1)} %copy.145) | copy-start | bytes 786436
  110.1 4.3 copy-start.19
  110.1 4.3 copy-start.24
  110.1 4.3 copy-start.56
  116.1 4.6 copy-start.31
  126.2 3.5 copy-start.22
  133.1 2.5 copy-start.32
  139.7 104.7 %reduce-scatter.2.cloned.1.call-start = ((), (), s32[]{:S(2)}) async-start(), calls=%async_computation.2 | async-start | bytes 5242880 | tf_op jit(solution)/shard_map/reduce_scatter | solution.py:158
  140.0 6.0 %copy-start.28 = (bf16[32,4,128,32]{2,3,1,0:T(8,128)(2,1)S(1)}, bf16[32,4,128,32]{2,3,1,0:T(8,128)(2,1)}, u32[]{:S(2)}) copy-start(bf16[32,4,128,32]{2,3,1,0:T(8,128)(2,1)} %fusion.70) | copy-start | bytes 3145732
  140.0 6.0 %copy-start.29 = (bf16[32,4,128,32]{2,3,1,0:T(8,128)(2,1)S(1)}, bf16[32,4,128,32]{2,3,1,0:T(8,128)(2,1)}, u32[]{:S(2)}) copy-start(bf16[32,4,128,32]{2,3,1,0:T(8,128)(2,1)} %fusion.67) | copy-start | bytes 3145732
  140.0 6.0 %copy-start.30 = (bf16[32,4,32,128]{3,2,1,0:T(8,128)(2,1)S(1)}, bf16[32,4,32,128]{3,2,1,0:T(8,128)(2,1)}, u32[]{:S(2)}) copy-start(bf16[32,4,32,128]{3,2,1,0:T(8,128)(2,1)} %fusion.168) | copy-start | bytes 3145732
  146.0 30.7 %copy-start.36 = (f32[32,128]{1,0:T(8,128)S(1)}, f32[32,128]{1,0:T(8,128)}, u32[]{:S(2)}) copy-start(f32[32,128]{1,0:T(8,128)} %copy-done.35) | copy-start | bytes 49156
  146.0 30.7 %copy-start.69 = (f32[128]{0:T(128)S(1)}, f32[128]{0:T(128)}, u32[]{:S(2)}) copy-start(f32[128]{0:T(128)} %param.25) | copy-start | bytes 1540
  146.0 30.7 %copy-start.72 = (bf16[128,4]{0,1:T(4,128)(2,1)S(1)}, bf16[128,4]{0,1:T(4,128)(2,1)}, u32[]{:S(2)}) copy-start(bf16[128,4]{0,1:T(4,128)(2,1)} %param.26) | copy-start | bytes 3076
  147.7 31.4 %copy-start.51 = (f32[32,128]{1,0:T(8,128)S(1)}, f32[32,128]{1,0:T(8,128)}, u32[]{:S(2)}) copy-start(f32[32,128]{1,0:T(8,128)} %copy-done.50) | copy-start | bytes 49156
  147.7 31.5 %copy-start.40 = (f32[32,128]{1,0:T(8,128)S(1)}, f32[32,128]{1,0:T(8,128)}, u32[]{:S(2)}) copy-start(f32[32,128]{1,0:T(8,128)} %copy-done.39) | copy-start | bytes 49156
  176.6 2.6 copy-start.9
  176.7 4.6 copy-start.20
  185.5 2.4 copy-start.15
  198.1 274.0 %all-reduce.16.cloned.1.call-start = ((), (), s32[]{:S(2)}) async-start(), calls=%async_computation.4 | async-start | bytes 1441792 | tf_op jit(solution)/shard_map/psum | solution.py:176
  199.6 3.7 copy-start.64
  203.6 2.4 copy-start.26
  206.0 5.3 %copy-start.7 = (f32[32,128,128]{1,2,0:T(8,128)S(1)}, f32[32,128,128]{1,2,0:T(8,128)}, u32[]{:S(2)}) copy-start(f32[32,128,128]{1,2,0:T(8,128)} %get-tuple-element.90) | copy-start | bytes 6291460
  213.1 2.3 copy-start.3
  213.1 3.0 copy-start.12
  216.0 28.3 %copy-start.45 = (f32[32,128]{1,0:T(8,128)S(1)}, f32[32,128]{1,0:T(8,128)}, u32[]{:S(2)}) copy-start(f32[32,128]{1,0:T(8,128)} %copy-done.43) | copy-start | bytes 49156
  217.2 32.2 %copy-start.53 = (bf16[128,512]{1,0:T(8,128)(2,1)S(1)}, bf16[128,512]{1,0:T(8,128)(2,1)}, u32[]{:S(2)}) copy-start(bf16[128,512]{1,0:T(8,128)(2,1)} %param.21) | copy-start | bytes 393220
  250.5 2.3 copy-start.59
  252.7 3.3 copy-start.47
  257.6 219.4 %copy-start.1 = (bf16[128,512]{1,0:T(8,128)(2,1)S(1)}, bf16[128,512]{1,0:T(8,128)(2,1)}, u32[]{:S(2)}) copy-start(bf16[128,512]{1,0:T(8,128)(2,1)} %param.27) | copy-start | bytes 393220
  (31 other events, 40.3 us)
Sparse Core Ops, SparseCore 0:
  16.1 50.2 all-gather.1
  139.8 36.7 all-reduce.13
  198.2 46.1 reduce-scatter.1
  327.2 144.9 all-reduce.15
where the time goes:
time: 493 us; the launch traced here: 484 us
  waiting for transfers between devices  248 us (50%)
  blocking collectives  71.1 us (14%)
  matrix products  66.1 us (13%)
  local copies, waits for them, and re-layouts  48.1 us (10%)
  other arithmetic  34.7 us (7%)
  between operations  15.6 us (3%)
    psum x1, waiting for transfers between devices, per_device(): summed_all = lax.psum(triangle_terms + attend_terms, ('dap', 'dp'))  144 us
    psum x1, blocking collectives, per_device(): summed_all = lax.psum(triangle_terms + attend_terms, ('dap', 'dp'))  65.8 us
    all_gather x1, waiting for transfers between devices, per_device(): right_all = lax.all_gather(right_proj, 'dap', axis=0, tiled=True)  47.5 us
    unnamed x5, waiting for transfers between devices  29 us
    reduce_scatter x1, waiting for transfers between devices, per_device(): lax.psum_scatter(jnp.einsum('ijc,ikc->jkc', d_product, left_proj, preferr...  27.1 us
    unnamed x158, local copies, waits for them, and re-layouts  19.1 us
    dot_general x3, matrix products, attend_second(): jnp.einsum('rjhd,rkhd->rhjk', query, keys_all, preferred_element_type=jnp...  11.1 us
    dot_general x3, matrix products, attend_second(): jnp.einsum('rhjk,rkhd->rjhd', weights, values_all, preferred_element_type...  10.3 us
  transfers between devices with their start and end apart: 4, of which 4 were waited for; matrix products, arithmetic and copies ran while one was open for 5% of the time, Pallas kernels for 0%

commit v1 on v0

v1 whole, which is shorter than its diff:
```python
from functools import partial

import jax
import jax.numpy as jnp
from jax import lax
from jax.experimental import pallas as pl
from jax.experimental.pallas import tpu as pltpu
from jax.sharding import PartitionSpec as P

EPSILON = 1e-05
MESH = pl.DeviceIdType.MESH
VM = pltpu.VMEM
DMA = pltpu.SemaphoreType.DMA
BF = jnp.bfloat16
F32 = jnp.float32
EXACT = lax.Precision.HIGHEST


def contract(x, y, dims, precision=None):
    return lax.dot_general(x, y, (dims, ((), ())), precision=precision, preferred_element_type=F32)


def mm(x, y, precision=None):
    return contract(x, y, ((1,), (0,)), precision)


def nt(x, y, precision=None):
    return contract(x, y, ((1,), (1,)), precision)


def tn(x, y, precision=None):
    return contract(x, y, ((0,), (0,)), precision)


def norm_cols(x):
    mean = jnp.sum(x, axis=0, keepdims=True) * (1.0 / 128)
    centred = x - mean
    spread = jnp.sum(centred * centred, axis=0, keepdims=True) * (1.0 / 128)
    scale = lax.rsqrt(spread + EPSILON)
    return centred * scale, scale


def norm_back(grad, unit, scale):
    a = jnp.sum(grad, axis=0, keepdims=True) * (1.0 / 128)
    b = jnp.sum(grad * unit, axis=0, keepdims=True) * (1.0 / 128)
    return scale * (grad - a - unit * b)


def loop(n, fn, unroll=1, first=0):
    def body(i, carry):
        fn(i)
        return carry
    lax.fori_loop(first, n, body, 0, unroll=unroll)


def at(i, size):
    return pl.ds(pl.multiple_of(i * size, size), size)


def halves(x):
    return x[:, :128], x[:, 128:]


def twice(x):
    return jnp.concatenate([x, x], axis=1)


def pair(ref, i):
    return jnp.concatenate([ref[i], ref[i + 1]], axis=1)


def lanes(r):
    return slice(128 * r, 128 * r + 128)


class Sum:
    def __init__(self, n_dp, factor, a, p, refs):
        self.n_dp, self.factor, self.a, self.p = n_dp, factor, a, p
        self.partner, self.cross = a + 1 - 2 * lax.rem(a, 2), lax.rem(a + 2, 4)
        (self.g, self.part, self.quarter, self.pieces, self.mine, self.joined, self.joined_b, self.full,
         self.sa, self.ra, self.sb, self.rb, self.sc, self.rc, self.sd, self.rd) = refs
        self.size = 256 // n_dp

    def remote(self, src, dst, s, r, **peer):
        return pltpu.make_async_remote_copy(
            src_ref=src, dst_ref=dst, send_sem=s, recv_sem=r, device_id=peer, device_id_type=MESH)

    def copy_a(self, r):
        peer = lax.rem(self.a + r, 4)
        return self.remote(self.g.at[at(peer, 256)], self.part.at[r - 1], self.sa.at[r - 1], self.ra.at[r - 1], dap=peer)

    def copy_b(self, r):
        peer = lax.rem(self.p + r, self.n_dp)
        return self.remote(
            self.quarter.at[at(peer, self.size)], self.pieces.at[r - 1], self.sb.at[r - 1], self.rb.at[r - 1], dp=peer)

    def copy_c(self, r, sending=True):
        peer = lax.rem(self.p + r, self.n_dp)
        owner = self.p if sending else lax.rem(self.p + self.n_dp - r, self.n_dp)
        return self.remote(
            self.mine, self.joined.at[at(owner, self.size)], self.sc.at[r - 1], self.rc.at[r - 1], dp=peer)

    def copy_d(self, k):
        there = at(self.cross if k == 2 else self.a, 256)
        src = self.full.at[there] if k == 2 else self.joined_b
        return self.remote(
            src, self.full.at[there], self.sd.at[k], self.rd.at[k], dap=self.cross if k == 0 else self.partner)

    def start_a(self):
        for r in (2, 1, 3):
            self.copy_a(r).start()

    def start_b(self):
        total = self.g[at(self.a, 256), :].astype(F32)
        for r in (1, 2, 3):
            self.copy_a(r).wait_recv()
            total = total + self.part[r - 1].astype(F32)
        self.quarter[...] = total
        loop(self.n_dp, lambda r: self.copy_b(r).start(), first=1)

    def start_c(self):
        loop(self.n_dp, lambda r: self.copy_b(r).wait_recv(), first=1)
        total = self.quarter[at(self.p, self.size), :] + jnp.sum(self.pieces[...], axis=0)
        self.mine[...] = total * self.factor
        loop(self.n_dp, lambda r: self.copy_c(r).start(), first=1)
        self.joined[at(self.p, self.size), :] = self.mine[...]

    def start_d(self):
        loop(self.n_dp, lambda r: self.copy_c(r, False).wait_recv(), first=1)
        self.joined_b[...] = self.joined[...].astype(BF)
        self.copy_d(0).start()
        self.copy_d(1).start()
        self.full[at(self.a, 256), :] = self.joined_b[...]

    def finish(self):
        self.copy_d(0).wait_recv()
        self.copy_d(2).start()
        self.copy_d(1).wait_recv()
        self.copy_d(2).wait_recv()

    def settle(self):
        for r in (1, 2, 3):
            self.copy_a(r).wait_send()
        loop(self.n_dp, lambda r: self.copy_b(r).wait_send(), first=1)
        loop(self.n_dp, lambda r: self.copy_c(r).wait_send(), first=1)
        for k in range(3):
            self.copy_d(k).wait_send()

    @staticmethod
    def scratch(n_dp):
        size = 256 // n_dp
        return [
            VM((1024, 128), BF), VM((3, 256, 128), BF), VM((256, 128), F32), VM((n_dp - 1, size, 128), F32),
            VM((size, 128), F32), VM((256, 128), F32), VM((256, 128), BF), VM((1024, 128), BF),
        ] + [DMA((3,))] * 2 + [DMA((n_dp - 1,))] * 4 + [DMA((3,))] * 2


N_IN, N_OUT, N_SUM = 15, 12, 16


def kernel(n_dp, factor, *refs):
    (slab, cot, tok_mask, tok_types, pair_mask, gain1, tri_in, tri_gate, gain2, tri_out, gain3, att_bias, att_in,
     att_out, table) = refs[:N_IN]
    (out, grad, o_gain1, o_tri_in, o_tri_gate, o_gain2, o_tri_out, o_gain3, o_att_bias, o_att_in, o_att_out,
     o_table) = refs[N_IN : N_IN + N_OUT]
    rest = refs[N_IN + N_OUT :]
    a, p = lax.axis_index("dap"), lax.axis_index("dp")
    partner, cross, chip, core = a + 1 - 2 * lax.rem(a, 2), lax.rem(a + 2, 4), a // 2, lax.rem(a, 2)
    early = Sum(n_dp, factor, a, p, rest[:N_SUM])
    late = Sum(n_dp, factor, a, p, rest[N_SUM : 2 * N_SUM])
    (live, live_t, tok_t, g1, g2, g3, w1, w1t, wat, wot, woutt, wb, wbt, hot, tab, bt,
     mid, dn3, prod, right, left_f, right_f, gates, pieces, normed, bias_f, bias_b, bias,
     d_bias, d_wa, d_wo, d_wout, d_wb, d_w1, gain_sum,
     db_n, db_in, db_f, d_prod, d_mid, d_gate, work, far, far_in, sent, cross_in, near, near_in,
     sem_es, sem_er, sem_is, sem_ir, sem_bs, sem_br, sem_s, sem_r) = rest[2 * N_SUM :]
    part = gates

    barrier = pltpu.get_barrier_semaphore()
    for r in range(1, 4):
        pl.semaphore_signal(barrier, inc=1, device_id={"dap": lax.rem(a + r, 4)}, device_id_type=MESH)
    loop(n_dp, lambda r: pl.semaphore_signal(
        barrier, inc=1, device_id={"dp": lax.rem(p + r, n_dp)}, device_id_type=MESH), first=1)

    rows_i = lax.broadcasted_iota(jnp.int32, (128, 128), 0)
    unit = (rows_i == lax.broadcasted_iota(jnp.int32, (128, 128), 1)).astype(F32).astype(BF)

    def flip(block):
        return nt(unit, block)

    def flipped(ref, i):
        return jnp.concatenate([flip(ref[i]), flip(ref[i + 1])], axis=1)

    def column(row):
        return jnp.broadcast_to(row, (128, 128)).T

    tokens = tok_mask[...].astype(F32)
    tok_t[...] = column(tokens)
    live[...] = pair_mask[...].astype(F32) * tok_t[at(a, 32), :] * tokens
    live_t[...] = tn(live[...].astype(BF), unit[:32, :32]).astype(BF)
    for gain, row in ((g1, gain1), (g2, gain2), (g3, gain3)):
        gain[...] = column(row[...])
    w1[:, 0:256] = tri_in[:, 0:256]
    w1[:, 256:384] = tri_gate[...]
    w1[:, 384:640] = tri_in[:, 256:512]
    for b in range(5):
        w1t[128 * b : 128 * b + 128, :] = flip(w1[:, lanes(b)]).astype(BF)
    for b in range(4):
        wat[128 * b : 128 * b + 128, :] = flip(att_in[:, lanes(b)]).astype(BF)
    wot[...] = flip(att_out[...]).astype(BF)
    woutt[...] = flip(tri_out[...]).astype(BF)
    wb[...] = jnp.zeros_like(wb)
    wb[:, 0:4] = att_bias[...]
    wbt[...] = tn(wb[...], unit).astype(BF)
    tab[...] = jnp.zeros_like(tab)
    tab[:, 0:4, 0:4] = table[...]
    hot[...] = (lax.broadcasted_iota(jnp.int32, (16, 128), 0) == tok_types[...]).astype(F32)

    def alive_of(i):
        return jnp.concatenate([live[pl.ds(i, 1), :], live[pl.ds(i + 1, 1), :]], axis=1)


    def edge(kind, c):
        spot = right.at[cross if kind == 2 else a, at(c, 8)]
        return pltpu.make_async_remote_copy(
            src_ref=spot, dst_ref=spot, send_sem=sem_es.at[kind, c], recv_sem=sem_er.at[kind, c],
            device_id={"dap": cross if kind == 1 else partner}, device_id_type=MESH)

    def project(c, t):
        i = c * 8 + 2 * t
        hat, _ = norm_cols(flipped(slab, i))
        n = (hat * twice(g1[...])).astype(BF)
        q = mm(w1t[...], n)
        alive = alive_of(i)
        sa, sb = jax.nn.sigmoid(q[128:256]), jax.nn.sigmoid(q[512:])
        lft = (sa * q[:128] * alive).astype(BF).astype(F32)
        rgt = (sb * q[384:512] * alive).astype(BF)
        gate = jax.nn.sigmoid(q[256:384])
        for r in range(2):
            normed[i + r] = n[:, lanes(r)]
            left_f[at(i + r, 128), :] = lft[:, lanes(r)]
            right[a, i + r] = rgt[:, lanes(r)]
            gates[i + r] = gate[:, lanes(r)]
            pieces[i + r, 0:128] = q[:128, lanes(r)]
            pieces[i + r, 128:256] = sa[:, lanes(r)]
            pieces[i + r, 256:384] = q[384:512, lanes(r)]
            pieces[i + r, 384:512] = sb[:, lanes(r)]

    def first(c):
        loop(4, lambda t: project(c, t))
        pl.when(c == 0)(lambda: pl.semaphore_wait(barrier, 3 + n_dp - 1))
        edge(1, c).start()
        edge(0, c).start()

    loop(4, first)

    def unpack(block, base):
        loop(32, lambda j: right_f.__setitem__((at(base + j, 128), slice(None)), right[block, j].astype(F32)), 2)

    def multiply(half):
        def one(ch):
            lft = left_f[pl.ds(ch, 32, stride=128), :].astype(BF)
            rgt = right_f[pl.ds(64 * 128 * half + ch, 64, stride=128), :].astype(BF)
            prod[at(ch, 32), 64 * half : 64 * half + 64] = nt(lft, rgt)
        loop(128, one, 4)

    loop(4, lambda c: edge(0, c).wait_recv())
    low = 2 * chip
    unpack(low, 0)
    unpack(low + 1, 32)
    multiply(0)

    def relay(c):
        edge(1, c).wait_recv()
        edge(2, c).start()

    loop(4, relay)
    loop(4, lambda c: edge(2, c).wait_recv())
    unpack(2 - low, 64)
    unpack(3 - low, 96)
    multiply(1)

    def second(t):
        i = 2 * t
        xs = []
        for r in range(2):
            rows = pl.ds(i + r, 128, stride=32)
            x = pltpu.roll(prod[rows, :], 64 * chip, axis=1)
            prod[rows, :] = x
            xs.append(x)
        hat, _ = norm_cols(jnp.concatenate(xs, axis=1))
        n = (hat * twice(g2[...])).astype(BF)
        middle = (flipped(slab, i) + pair(gates, i) * mm(woutt[...], n)).astype(BF)
        hat, _ = norm_cols(middle.astype(F32))
        n = (hat * twice(g3[...])).astype(BF)
        heads = mm(wbt[...], n)
        for r in range(2):
            mid[i + r] = middle[:, lanes(r)]
            for h in range(4):
                bias_f[h, pl.ds(i + r, 1), :] = heads[h : h + 1, lanes(r)]

    loop(16, second)
    bias_b[...] = bias_f[...].astype(BF)

    def share_bias(r):
        return pltpu.make_async_remote_copy(
            src_ref=bias_b, dst_ref=bias.at[:, at(a, 32), :], send_sem=sem_is.at[r - 1], recv_sem=sem_ir.at[r - 1],
            device_id={"dap": lax.rem(a + r, 4)}, device_id_type=MESH)

    for r in (2, 1, 3):
        share_bias(r).start()
    bias[:, at(a, 32), :] = bias_b[...]
    for h in range(4):
        near_types = mm(tab[h].T, hot[...], EXACT)
        bt[:, lanes(h)] = tn(hot[...], near_types, EXACT)
    for ref in (d_bias, d_wa, d_wo, d_wout, d_wb, d_w1, gain_sum):
        ref[...] = jnp.zeros_like(ref)
    for r in (1, 2, 3):
        share_bias(r).wait_recv()
    for h in range(4):
        bt[:, lanes(h)] += flip(bias[h])


    def spread(x):
        zero = jnp.zeros((32, 128), x.dtype)
        cols = [
            jnp.concatenate([x[32 * h : 32 * h + 32] if g == h else zero for g in range(4)], axis=0)
            for h in range(4)
        ]
        return jnp.concatenate(cols, axis=1)

    scale = 32.0 ** -0.5

    def attend(t):
        i = 2 * t
        m = pair(mid, i).astype(F32)
        hat, _ = norm_cols(m)
        n = (hat * twice(g3[...])).astype(BF)
        q3 = mm(wat[...], n)
        qkv = q3[:384].astype(BF)
        gate = jax.nn.sigmoid(q3[384:])
        ct = flipped(cot, i).astype(BF)
        d_gated = mm(att_out[...], ct).astype(BF).astype(F32)
        d_att = d_gated * gate
        picked = lax.broadcasted_iota(jnp.int32, (32, 256), 0) == (
            i + lax.broadcasted_iota(jnp.int32, (32, 256), 1) // 128)
        alive = mm(live_t[...], picked.astype(F32).astype(BF))
        parts, atts = [], []
        for r in range(2):
            q, k, v = (qkv[128 * x : 128 * x + 128, lanes(r)] for x in range(3))
            kv = flip(qkv[128:384, lanes(r)]).astype(BF)
            q4 = spread(q)
            e = jnp.exp(mm(kv[:, :128], q4) * scale + bt[...])
            e = e * jnp.concatenate([alive[:, lanes(r)]] * 4, axis=1)
            s = jnp.sum(e, axis=0, keepdims=True)
            w = e * (1.0 / jnp.maximum(s, 1.0))
            ab = w.astype(BF)
            atts.append(jnp.concatenate([mm(v[32 * h : 32 * h + 32], ab[:, lanes(h)]) for h in range(4)], axis=0))
            do4 = spread(d_att[:, lanes(r)].astype(BF))
            da = mm(kv[:, 128:], do4).astype(BF).astype(F32)
            u = da * w
            total = jnp.sum(u, axis=0, keepdims=True)
            total = jnp.where(s > 1.0, total, jnp.where(s == 1.0, 0.5 * total, 0.0))
            ds = u - w * total
            d_bias[...] += ds
            dsb = ds.astype(BF)
            dv = nt(do4, ab)
            dk = nt(q4, dsb) * scale
            dq = jnp.concatenate(
                [mm(k[32 * h : 32 * h + 32], dsb[:, lanes(h)]) for h in range(4)], axis=0) * scale
            parts.append(jnp.concatenate([dq, dk, dv], axis=0).astype(BF))
        att = jnp.concatenate(atts, axis=1)
        d_open = (d_gated * att * gate * (1.0 - gate)).astype(BF)
        dp = jnp.concatenate([jnp.concatenate(parts, axis=1), d_open], axis=0)
        dn = mm(att_in[...], dp).astype(BF)
        d_wa[...] += nt(dp, n)
        gated = (gate * att).astype(BF)
        d_wo[...] += nt(gated, ct)
        res = (m + mm(wot[...], gated)).astype(BF)
        for r in range(2):
            dn3[i + r] = dn[:, lanes(r)]
            out[i + r] = flip(res[:, lanes(r)]).astype(BF)

    loop(16, attend)

    for h in range(4):
        db_n[h] = flip(d_bias[:, lanes(h)].astype(BF)).astype(BF)

    def share_grad(r):
        peer = lax.rem(a + r, 4)
        return pltpu.make_async_remote_copy(
            src_ref=db_n.at[:, at(peer, 32), :], dst_ref=db_in.at[r - 1], send_sem=sem_bs.at[r - 1],
            recv_sem=sem_br.at[r - 1], device_id={"dap": peer}, device_id_type=MESH)

    for r in (2, 1, 3):
        share_grad(r).start()
    early.g[0:512, :] = d_wa[...].astype(BF)
    early.g[512:640, :] = d_wo[...].astype(BF)
    early.g[640:, :] = jnp.zeros((384, 128), BF)
    for h in range(4):
        near_types = mm(hot[...], d_bias[:, lanes(h)])
        early.g[640 + 16 * h : 656 + 16 * h, 0:16] = nt(hot[...], near_types).astype(BF)
    early.start_a()

    for r in (1, 2, 3):
        share_grad(r).wait_recv()
    total = db_n[:, at(a, 32), :].astype(F32)
    for r in range(3):
        total = total + db_in[r].astype(F32)
    db_f[...] = total


    def fold(x):
        return x[:, :128] + x[:, 128:]

    def second_back(t):
        i = 2 * t
        hat3, scale3 = norm_cols(pair(mid, i).astype(F32))
        gain3, gain2 = twice(g3[...]), twice(g2[...])
        n3 = (hat3 * gain3).astype(BF)
        rows = [
            jnp.concatenate([db_f[h, pl.ds(i, 1), :], db_f[h, pl.ds(i + 1, 1), :]], axis=1) for h in range(4)
        ]
        db = jnp.concatenate(rows + [jnp.zeros((12, 256), F32)], axis=0).astype(BF)
        dn = pair(dn3, i).astype(F32) + mm(wb[...], db)
        d_wb[...] += nt(db, n3)
        gain_sum[2] += fold(dn * hat3)
        dm = flipped(cot, i).astype(BF) + norm_back(dn * gain3, hat3, scale3).astype(BF)
        dmf = dm.astype(F32)
        x = jnp.concatenate([prod[pl.ds(i, 128, stride=32), :], prod[pl.ds(i + 1, 128, stride=32), :]], axis=1)
        hat2, scale2 = norm_cols(x)
        n2 = (hat2 * gain2).astype(BF)
        z = mm(woutt[...], n2)
        gate = pair(gates, i)
        dz = (dmf * gate).astype(BF)
        d_open = (dmf * z * gate * (1.0 - gate)).astype(BF)
        d_wout[...] += nt(n2, dz)
        dn2 = mm(tri_out[...], dz).astype(BF).astype(F32)
        gain_sum[1] += fold(dn2 * hat2)
        dp = norm_back(dn2 * gain2, hat2, scale2)
        for r in range(2):
            d_prod[pl.ds(i + r, 128, stride=32), :] = pltpu.roll(dp[:, lanes(r)], 64 * chip, axis=1)
            d_mid[i + r] = dm[:, lanes(r)]
            d_gate[i + r] = d_open[:, lanes(r)]

    loop(16, second_back)
    early.start_b()

    def chunk(ref, q):
        return ref.at[:, at(q, 32), :]

    def move(kind, q):
        src, dst, peer = (
            (far.at[1 - core], far_in, partner), (sent, cross_in, cross), (near.at[1 - core], near_in, partner),
        )[kind]
        return pltpu.make_async_remote_copy(
            src_ref=chunk(src, q), dst_ref=chunk(dst, q), send_sem=sem_s.at[kind, q], recv_sem=sem_r.at[kind, q],
            device_id={"dap": peer}, device_id_type=MESH)

    def right_grads(half, q, store):
        def one(c):
            ch = 32 * q + c
            dp = d_prod[at(ch, 32), 64 * half : 64 * half + 64].astype(BF)
            work[pl.ds(c, 64, stride=32), :] = tn(dp, left_f[pl.ds(ch, 32, stride=128), :].astype(BF))

        loop(32, one, 4)

        def pack(j):
            store[j // 32, lax.rem(j, 32), at(q, 32), :] = work[at(j, 32), :].astype(BF)

        loop(64, pack, 4)

    def add_on(q):
        move(0, q).wait_recv()

        def one(j):
            spot = at(q, 32)
            sent[j, spot, :] = (far[core, j, spot, :].astype(F32) + far_in[j, spot, :].astype(F32)).astype(BF)

        loop(32, one, 4)
        move(1, q).start()

    def out_far(q):
        right_grads(1, q, far)
        move(0, q).start()
        pl.when(q > 0)(lambda: add_on(q - 1))

    loop(4, out_far)

    def out_near(q):
        right_grads(0, q, near)
        move(2, q).start()
        pl.when(q == 0)(lambda: add_on(3))

    loop(4, out_near)
    early.start_c()

    def left_grad(ch):
        rgt = right_f[pl.ds(ch, 128, stride=128), :].astype(BF)
        left_f[pl.ds(ch, 32, stride=128), :] = mm(d_prod[at(ch, 32), :].astype(BF), rgt)

    loop(128, left_grad, 4)

    def sides(grad_in, x, s, alive):
        g = grad_in * alive * s
        return g, g * x * (1.0 - s)

    def stored(i, k):
        rows = slice(128 * k, 128 * k + 128)
        return jnp.concatenate([pieces[i, rows], pieces[i + 1, rows]], axis=1)

    def left_part(t):
        i = 2 * t
        dl = jnp.concatenate([left_f[at(i, 128), :], left_f[at(i + 1, 128), :]], axis=1).astype(BF).astype(F32)
        dpa, dga = sides(dl, stored(i, 0), stored(i, 1), alive_of(i))
        dp = jnp.concatenate([dpa.astype(BF), dga.astype(BF), pair(d_gate, i)], axis=0)
        d_w1[0:384, :] += nt(dp, pair(normed, i))
        dn = mm(w1[:, 0:384], dp)
        part[i] = dn[:, :128]
        part[i + 1] = dn[:, 128:]

    loop(16, left_part)

    loop(4, lambda q: move(2, q).wait_recv())
    loop(4, lambda q: move(1, q).wait_recv())
    early.start_d()

    def right_part(t):
        i = 2 * t

        def summed(j):
            x = near[core, j].astype(F32) + near_in[j].astype(F32) + cross_in[j].astype(F32)
            return x.astype(BF).astype(F32)

        dr = jnp.concatenate([summed(i), summed(i + 1)], axis=1)
        dpb, dgb = sides(dr, stored(i, 2), stored(i, 3), alive_of(i))
        dp = jnp.concatenate([dpb.astype(BF), dgb.astype(BF)], axis=0)
        d_w1[384:640, :] += nt(dp, pair(normed, i))
        dn = (pair(part, i) + mm(w1[:, 384:640], dp)).astype(BF).astype(F32)
        hat, spread_1 = norm_cols(flipped(slab, i))
        gain_sum[0] += fold(dn * hat)
        dx = norm_back(dn * twice(g1[...]), hat, spread_1).astype(BF)
        res = pair(d_mid, i) + dx
        grad[i] = flip(res[:, :128]).astype(BF)
        grad[i + 1] = flip(res[:, 128:]).astype(BF)

    loop(16, right_part)


    late.g[0:640, :] = d_w1[...].astype(BF)
    late.g[640:768, :] = d_wout[...].astype(BF)
    late.g[768:784, :] = d_wb[...].astype(BF)
    late.g[784:, :] = jnp.zeros((240, 128), BF)
    ones = jnp.ones((16, 128), F32)
    for k in range(3):
        late.g[784 + 16 * k : 800 + 16 * k, :] = nt(ones, gain_sum[k], EXACT).astype(BF)
    late.start_a()
    early.finish()
    for b in range(4):
        o_att_in[:, lanes(b)] = flip(early.full[128 * b : 128 * b + 128, :])
    o_att_out[...] = early.full[512:640, :].astype(F32)
    for h in range(4):
        o_table[h] = early.full[640 + 16 * h : 656 + 16 * h, :].astype(F32)[0:4, 0:4]
    late.start_b()
    early.settle()
    late.start_c()
    for r in (1, 2, 3):
        share_bias(r).wait_send()
        share_grad(r).wait_send()
    for kind in range(3):
        loop(4, lambda c: edge(kind, c).wait_send())
        loop(4, lambda q: move(kind, q).wait_send())
    late.start_d()
    late.finish()
    for b, source in enumerate((0, 1, 3, 4)):
        o_tri_in[:, lanes(b)] = flip(late.full[128 * source : 128 * source + 128, :])
    o_tri_gate[...] = flip(late.full[256:384, :])
    o_tri_out[...] = late.full[640:768, :].astype(F32)
    o_att_bias[...] = flip(jnp.concatenate([late.full[768:784, :], jnp.zeros((112, 128), BF)], axis=0))[:, 0:4]
    for k, ref in enumerate((o_gain1, o_gain2, o_gain3)):
        ref[...] = late.full[784 + 16 * k : 800 + 16 * k, :].astype(F32)[0:1, :]
    late.settle()


def per_device(*args):
    pair_rep, cotangent, tok_mask, tok_types, pair_mask = args[:5]
    params = [v[None] if v.ndim == 1 else v for v in args[5:]]
    n_dp = lax.axis_size("dp")
    factor = (128 * 128 * n_dp) ** (-0.5)
    block = (32, 128, 128)
    shapes = [v.shape for v in params]
    spec = pl.BlockSpec(memory_space=VM)
    scratch = Sum.scratch(n_dp) * 2 + [
        VM((32, 128), F32), VM((128, 32), BF), VM((128, 128), F32),
        VM((128, 128), F32), VM((128, 128), F32), VM((128, 128), F32),
        VM((128, 640), BF), VM((640, 128), BF), VM((512, 128), BF), VM((128, 128), BF), VM((128, 128), BF),
        VM((128, 16), BF), VM((16, 128), BF), VM((16, 128), F32), VM((4, 16, 16), F32), VM((128, 512), F32),
        VM(block, BF), VM(block, BF), VM((4096, 128), F32), VM((4,) + block, BF), VM((4096, 128), F32),
        VM((16384, 128), F32), VM(block, F32), VM((32, 512, 128), F32), VM(block, BF),
        VM((4, 32, 128), F32), VM((4, 32, 128), BF), VM((4, 128, 128), BF),
        VM((128, 512), F32), VM((512, 128), F32), VM((128, 128), F32), VM((128, 128), F32), VM((16, 128), F32),
        VM((640, 128), F32), VM((3, 128, 128), F32),
        VM((4, 128, 128), BF), VM((3, 4, 32, 128), BF), VM((4, 32, 128), F32), VM((4096, 128), F32),
        VM(block, BF), VM(block, BF), VM((2048, 128), F32),
        VM((2,) + block, BF), VM(block, BF), VM(block, BF), VM(block, BF), VM((2,) + block, BF), VM(block, BF),
        DMA((3, 4)), DMA((3, 4)), DMA((3,)), DMA((3,)), DMA((3,)), DMA((3,)), DMA((3, 4)), DMA((3, 4)),
    ]
    results = pl.pallas_call(
        partial(kernel, n_dp, factor),
        out_shape=[jax.ShapeDtypeStruct(block, BF)] * 2 + [jax.ShapeDtypeStruct(s, F32) for s in shapes],
        in_specs=[spec] * N_IN,
        out_specs=[spec] * N_OUT,
        scratch_shapes=scratch,
        compiler_params=pltpu.CompilerParams(collective_id=0, has_side_effects=True, vmem_limit_bytes=63 << 20),
        name="pairformer",
    )(pair_rep[0], cotangent[0], tok_mask, tok_types, pair_mask[0], *params)
    return tuple(
        [results[0][None], results[1][None]]
        + [r[0] if v.ndim == 1 else r for r, v in zip(results[2:], args[5:])]
    )


def solution(mesh):
    return jax.shard_map(
        per_device,
        mesh=mesh,
        in_specs=(
            P("dp", "dap", None, None),
            P("dp", "dap", None, None),
            P("dp", None),
            P("dp", None),
            P("dp", "dap", None),
            P(),
            P(),
            P(),
            P(),
            P(),
            P(),
            P(),
            P(),
            P(),
            P(),
        ),
        out_specs=(
            P("dp", "dap", None, None),
            P("dp", "dap", None, None),
            P(),
            P(),
            P(),
            P(),
            P(),
            P(),
            P(),
            P(),
            P(),
            P(),
        ),
        check_vma=False,
    )
```

time: 493 us -> 196 us (0.40); the launches traced: 484 us -> 195 us
  waiting for transfers between devices: 248 us -> 0 us
  Pallas kernels: 0 us -> 182 us
  blocking collectives: 71.1 us -> 0 us
  matrix products: 66.1 us -> 0 us
  local copies, waits for them, and re-layouts: 48.1 us -> 12.1 us
  other arithmetic: 34.7 us -> 0 us
  between operations: 15.6 us -> 0.68 us
    pallas_call x0 -> x1, Pallas kernels: none -> 182 us  [per_device(): pl.pallas_call(partial(kernel, n_dp, factor), out_shape=[jax.ShapeDtypeSt...]
    psum x1 -> x0, waiting for transfers between devices: 144 us -> none  [per_device(): summed_all = lax.psum(triangle_terms + attend_terms, ('dap', 'dp'))]
    dot_general x29 -> x0, matrix products: 66 us -> none  [the longest x3 11.1 us: attend_second(): jnp.einsum('rjhd,rkhd->rhjk', query, keys_all, preferred_element_type=jnp...]
    psum x1 -> x0, blocking collectives: 65.8 us -> none  [per_device(): summed_all = lax.psum(triangle_terms + attend_terms, ('dap', 'dp'))]
    all_gather x1 -> x0, waiting for transfers between devices: 47.5 us -> none  [per_device(): right_all = lax.all_gather(right_proj, 'dap', axis=0, tiled=True)]
    unnamed x5 -> x0, waiting for transfers between devices: 29 us -> none
    reduce_scatter x1 -> x0, waiting for transfers between devices: 27.1 us -> none  [per_device(): lax.psum_scatter(jnp.einsum('ijc,ikc->jkc', d_product, left_proj, preferr...]
    mul x11 -> x0, other arithmetic: 16.2 us -> none  [the longest x1 5.08 us: triangle_first(): jax.nn.sigmoid(projected[..., 3 * channels:])]
  transfers between devices with their start and end apart: 4 -> 0, of which waited for: 4 -> 0; matrix products, arithmetic and copies ran while one was open for 5% -> 0% of each run, Pallas kernels for 0% -> 0%
where the time goes in v1:
time: 196 us; the launch traced here: 195 us
  Pallas kernels  182 us (93%)
  local copies, waits for them, and re-layouts  12.1 us (6%)
    pallas_call x1, Pallas kernels, per_device(): pl.pallas_call(partial(kernel, n_dp, factor), out_shape=[jax.ShapeDtypeSt...  182 us
    unnamed x35, local copies, waits for them, and re-layouts  12.1 us

profile of v1, /device:TPU:1, one launch (start us, length us, event | category | flops | bytes accessed | tf_op | source)
XLA Modules:
  0.0 195.3 jit_solution(3509774139168334354)
XLA Ops:
  0.6 0.0 copy-start.7
  0.7 0.7 copy-done.7
  1.3 0.7 copy.27.refs_11_
  2.1 182.5 %pairformer.1 = (bf16[32,128,128]{2,1,0:T(8,128)(2,1)}, bf16[32,128,128]{2,1,0:T(8,128)(2,1)}, f32[1,128]{1,0:T(1,128)}, f32[128,512]{1,0:T(8,128)}, f32[128,128...) custom-call(bf16[32,128,128]{2,1,0:T(8,128)(2,1)} %bitcast.11, ...), custom_call_target="tpu_custom_call" | custom-call | tf_op jit(solution)/shard_map/pairformer/pallas_call | solution.py:607
  184.6 1.5 copy.28
  186.1 0.0 copy-start
  186.1 2.4 %copy.40 = bf16[1,32,128,128]{3,2,1,0:T(8,128)(2,1)} copy(bf16[1,32,128,128]{3,2,1,0:T(8,128)(2,1)} %bitcast.14) | data formatting | bytes 2097152
  188.4 0.0 copy-done
  188.4 0.0 copy-start.10
  188.5 0.0 copy-start.2
  188.5 1.0 copy.41
  189.4 0.0 copy-done.10
  189.4 0.5 copy.42
  189.9 0.0 copy-done.2
  189.9 0.0 copy-start.5
  189.9 0.0 copy-start.9
  189.9 0.0 copy-start.4
  190.0 0.7 copy.43
  190.7 0.1 copy-done.5
  190.8 0.0 copy-start.1
  190.8 0.6 copy.44
  191.4 0.0 copy-done.9
  191.4 0.5 copy.45
  191.9 0.0 copy-done.4
  191.9 0.0 copy-start.8
  191.9 0.6 copy.46
  192.6 0.0 copy-done.8
  192.6 0.5 copy.47
  193.1 0.0 copy-done.1
  193.1 0.0 copy-start.3
  193.1 0.7 copy.48
  193.8 0.2 copy-done.3
  194.0 0.0 copy-start.6
  194.0 0.6 copy.49
  194.6 0.1 copy-done.6
  194.7 0.6 copy.50
Async XLA Ops:
  0.6 0.7 copy-start.7
  186.1 2.4 %copy-start = (bf16[32,128,128]{2,1,0:T(8,128)(2,1)S(1)}, bf16[32,128,128]{2,1,0:T(8,128)(2,1)}, u32[]{:S(2)}) copy-start(bf16[32,128,128]{2,1,0:T(8,128)(2,1)} %get-tuple-element.25) | copy-start | bytes 3145732
  188.4 1.0 copy-start.10
  188.5 1.5 copy-start.2
  189.9 0.8 copy-start.5
  189.9 1.5 copy-start.9
  189.9 2.0 %copy-start.4 = (f32[128,128]{1,0:T(8,128)S(1)}, f32[128,128]{1,0:T(8,128)}, u32[]{:S(2)}) copy-start(f32[128,128]{1,0:T(8,128)} %get-tuple-element.66) | copy-start | bytes 196612
  190.8 2.3 %copy-start.1 = (f32[128,512]{1,0:T(8,128)S(1)}, f32[128,512]{1,0:T(8,128)}, u32[]{:S(2)}) copy-start(f32[128,512]{1,0:T(8,128)} %get-tuple-element.69) | copy-start | bytes 786436
  191.9 0.7 copy-start.8
  193.1 0.9 copy-start.3
  194.0 0.7 copy-start.6

commit v2 on v1

--- a/solution.py
+++ b/solution.py
@@ -208,9 +208,8 @@
         wat[128 * b : 128 * b + 128, :] = flip(att_in[:, lanes(b)]).astype(BF)
     wot[...] = flip(att_out[...]).astype(BF)
     woutt[...] = flip(tri_out[...]).astype(BF)
-    wb[...] = jnp.zeros_like(wb)
-    wb[:, 0:4] = att_bias[...]
-    wbt[...] = tn(wb[...], unit).astype(BF)
+    wbt[...] = jnp.concatenate([att_bias[...].astype(F32), jnp.zeros((12, 128), F32)], axis=0).astype(BF)
+    wb[...] = flip(wbt[...]).astype(BF)
     tab[...] = jnp.zeros_like(tab)
     tab[:, 0:4, 0:4] = table[...]
     hot[...] = (lax.broadcasted_iota(jnp.int32, (16, 128), 0) == tok_types[...]).astype(F32)
@@ -246,7 +245,7 @@
             pieces[i + r, 384:512] = sb[:, lanes(r)]
 
     def first(c):
-        loop(4, lambda t: project(c, t))
+        loop(4, lambda t: project(c, t), 2)
         pl.when(c == 0)(lambda: pl.semaphore_wait(barrier, 3 + n_dp - 1))
         edge(1, c).start()
         edge(0, c).start()
@@ -261,7 +260,7 @@
             lft = left_f[pl.ds(ch, 32, stride=128), :].astype(BF)
             rgt = right_f[pl.ds(64 * 128 * half + ch, 64, stride=128), :].astype(BF)
             prod[at(ch, 32), 64 * half : 64 * half + 64] = nt(lft, rgt)
-        loop(128, one, 4)
+        loop(128, one, 16)
 
     loop(4, lambda c: edge(0, c).wait_recv())
     low = 2 * chip
@@ -298,7 +297,7 @@
             for h in range(4):
                 bias_f[h, pl.ds(i + r, 1), :] = heads[h : h + 1, lanes(r)]
 
-    loop(16, second)
+    loop(16, second, 4)
     bias_b[...] = bias_f[...].astype(BF)
 
     def share_bias(r):
@@ -380,7 +379,7 @@
             dn3[i + r] = dn[:, lanes(r)]
             out[i + r] = flip(res[:, lanes(r)]).astype(BF)
 
-    loop(16, attend)
+    loop(16, attend, 2)
 
     for h in range(4):
         db_n[h] = flip(d_bias[:, lanes(h)].astype(BF)).astype(BF)
@@ -442,7 +441,7 @@
             d_mid[i + r] = dm[:, lanes(r)]
             d_gate[i + r] = d_open[:, lanes(r)]
 
-    loop(16, second_back)
+    loop(16, second_back, 4)
     early.start_b()
 
     def chunk(ref, q):
@@ -462,7 +461,7 @@
             dp = d_prod[at(ch, 32), 64 * half : 64 * half + 64].astype(BF)
             work[pl.ds(c, 64, stride=32), :] = tn(dp, left_f[pl.ds(ch, 32, stride=128), :].astype(BF))
 
-        loop(32, one, 4)
+        loop(32, one, 16)
 
         def pack(j):
             store[j // 32, lax.rem(j, 32), at(q, 32), :] = work[at(j, 32), :].astype(BF)
@@ -498,7 +497,7 @@
         rgt = right_f[pl.ds(ch, 128, stride=128), :].astype(BF)
         left_f[pl.ds(ch, 32, stride=128), :] = mm(d_prod[at(ch, 32), :].astype(BF), rgt)
 
-    loop(128, left_grad, 4)
+    loop(128, left_grad, 16)
 
     def sides(grad_in, x, s, alive):
         g = grad_in * alive * s
@@ -518,7 +517,7 @@
         part[i] = dn[:, :128]
         part[i + 1] = dn[:, 128:]
 
-    loop(16, left_part)
+    loop(16, left_part, 4)
 
     loop(4, lambda q: move(2, q).wait_recv())
     loop(4, lambda q: move(1, q).wait_recv())
@@ -543,7 +542,7 @@
         grad[i] = flip(res[:, :128]).astype(BF)
         grad[i + 1] = flip(res[:, 128:]).astype(BF)
 
-    loop(16, right_part)
+    loop(16, right_part, 4)
 
 
     late.g[0:640, :] = d_w1[...].astype(BF)
@@ -575,15 +574,31 @@
         o_tri_in[:, lanes(b)] = flip(late.full[128 * source : 128 * source + 128, :])
     o_tri_gate[...] = flip(late.full[256:384, :])
     o_tri_out[...] = late.full[640:768, :].astype(F32)
-    o_att_bias[...] = flip(jnp.concatenate([late.full[768:784, :], jnp.zeros((112, 128), BF)], axis=0))[:, 0:4]
+    o_att_bias[...] = late.full[768:784, :].astype(F32)[0:4, :]
     for k, ref in enumerate((o_gain1, o_gain2, o_gain3)):
         ref[...] = late.full[784 + 16 * k : 800 + 16 * k, :].astype(F32)[0:1, :]
     late.settle()
 
 
+def hand_over(*refs):
+    held, sems = refs[2 * N_OUT : 3 * N_OUT], refs[3 * N_OUT]
+    parts = [(k, pl.ds(8 * c, 8), 4 * k + c) for k in range(2) for c in range(4)]
+    parts += [(k, slice(None), 6 + k) for k in range(2, N_OUT)]
+    reads = [pltpu.make_async_copy(refs[k].at[s], held[k].at[s], sems.at[0, n]) for k, s, n in parts]
+    writes = [pltpu.make_async_copy(held[k].at[s], refs[N_OUT + k].at[s], sems.at[1, n]) for k, s, n in parts]
+    for copy in reads:
+        copy.start()
+    for read, write in zip(reads, writes):
+        read.wait()
+        write.start()
+    for copy in writes:
+        copy.wait()
+
+
 def per_device(*args):
     pair_rep, cotangent, tok_mask, tok_types, pair_mask = args[:5]
     params = [v[None] if v.ndim == 1 else v for v in args[5:]]
+    params[6] = params[6].T
     n_dp = lax.axis_size("dp")
     factor = (128 * 128 * n_dp) ** (-0.5)
     block = (32, 128, 128)
@@ -613,6 +628,17 @@
         compiler_params=pltpu.CompilerParams(collective_id=0, has_side_effects=True, vmem_limit_bytes=63 << 20),
         name="pairformer",
     )(pair_rep[0], cotangent[0], tok_mask, tok_types, pair_mask[0], *params)
+    anywhere = pl.BlockSpec(memory_space=pl.ANY)
+    results = pl.pallas_call(
+        hand_over,
+        out_shape=[jax.ShapeDtypeStruct(r.shape, r.dtype) for r in results],
+        in_specs=[anywhere] * N_OUT,
+        out_specs=[anywhere] * N_OUT,
+        scratch_shapes=[VM(r.shape, r.dtype) for r in results] + [DMA((2, N_OUT + 6))],
+        name="hand_over",
+    )(*results)
+    results = list(results)
+    results[8] = results[8].T
     return tuple(
         [results[0][None], results[1][None]]
         + [r[0] if v.ndim == 1 else r for r, v in zip(results[2:], args[5:])]

time: 196 us -> 163 us (0.83)
  Pallas kernels: 182 us -> 162 us
  local copies, waits for them, and re-layouts: 12.1 us -> 0 us
    pallas_call x1, Pallas kernels: 182 us -> 159 us  [per_device(): pl.pallas_call(partial(kernel, n_dp, factor), out_shape=[jax.ShapeDtypeSt...]
    unnamed x35 -> x0, local copies, waits for them, and re-layouts: 12.1 us -> none
    pallas_call x0 -> x1, Pallas kernels: none -> 2.83 us  [per_device(): pl.pallas_call(hand_over, out_shape=[jax.ShapeDtypeStruct(r.shape, r.dtyp...]
where the time goes in v2:
time: 163 us
  Pallas kernels  162 us (99%)
    pallas_call x1, Pallas kernels, per_device(): pl.pallas_call(partial(kernel, n_dp, factor), out_shape=[jax.ShapeDtypeSt...  159 us

profile of v2, /device:TPU:1, one launch (start us, length us, event | category | flops | bytes accessed | tf_op | source)
XLA Modules:
  0.0 162.8 jit_solution(15540231733626793827)
XLA Ops:
  0.7 159.3 %pairformer.1 = (bf16[32,128,128]{2,1,0:T(8,128)(2,1)}, bf16[32,128,128]{2,1,0:T(8,128)(2,1)}, f32[1,128]{1,0:T(1,128)}, f32[128,512]{1,0:T(8,128)}, f32[128,128...) custom-call(bf16[32,128,128]{2,1,0:T(8,128)(2,1)} %bitcast.13, ...), custom_call_target="tpu_custom_call" | custom-call | tf_op jit(solution)/shard_map/pairformer/pallas_call | solution.py:622
  159.9 2.8 %hand_over.1 = (bf16[32,128,128]{2,1,0:T(8,128)(2,1)}, bf16[32,128,128]{2,1,0:T(8,128)(2,1)}, f32[1,128]{1,0:T(1,128)}, f32[128,512]{1,0:T(8,128)}, f32[128,128]...) custom-call(bf16[32,128,128]{2,1,0:T(8,128)(2,1)} %get-tuple-element, ...), custom_call_target="tpu_custom_call" | custom-call | tf_op jit(solution)/shard_map/hand_over/pallas_call | solution.py:632

commit v3 on v2

--- a/solution.py
+++ b/solution.py
@@ -92,13 +92,17 @@
     def copy_b(self, r):
         peer = lax.rem(self.p + r, self.n_dp)
         return self.remote(
-            self.quarter.at[at(peer, self.size)], self.pieces.at[r - 1], self.sb.at[r - 1], self.rb.at[r - 1], dp=peer)
-
-    def copy_c(self, r, sending=True):
+            self.quarter.at[at(peer, self.size)], self.pieces.at[r - 1], self.sb, self.rb, dp=peer)
+
+    def copy_c(self, r):
         peer = lax.rem(self.p + r, self.n_dp)
-        owner = self.p if sending else lax.rem(self.p + self.n_dp - r, self.n_dp)
-        return self.remote(
-            self.mine, self.joined.at[at(owner, self.size)], self.sc.at[r - 1], self.rc.at[r - 1], dp=peer)
+        return self.remote(self.mine, self.joined.at[at(self.p, self.size)], self.sc, self.rc, dp=peer)
+
+    def all_of(self, ref, s, r):
+        return self.remote(ref, ref, s, r, dp=lax.rem(self.p + 1, self.n_dp))
+
+    def others(self, ref):
+        return ref.at[pl.ds(0, (self.n_dp - 1) * self.size)]
 
     def copy_d(self, k):
         there = at(self.cross if k == 2 else self.a, 256)
@@ -116,17 +120,19 @@
             self.copy_a(r).wait_recv()
             total = total + self.part[r - 1].astype(F32)
         self.quarter[...] = total
-        loop(self.n_dp, lambda r: self.copy_b(r).start(), first=1)
+        for r in range(1, self.n_dp):
+            self.copy_b(r).start()
 
     def start_c(self):
-        loop(self.n_dp, lambda r: self.copy_b(r).wait_recv(), first=1)
+        self.all_of(self.pieces, self.sb, self.rb).wait_recv()
         total = self.quarter[at(self.p, self.size), :] + jnp.sum(self.pieces[...], axis=0)
         self.mine[...] = total * self.factor
-        loop(self.n_dp, lambda r: self.copy_c(r).start(), first=1)
+        for r in range(1, self.n_dp):
+            self.copy_c(r).start()
         self.joined[at(self.p, self.size), :] = self.mine[...]
 
     def start_d(self):
-        loop(self.n_dp, lambda r: self.copy_c(r, False).wait_recv(), first=1)
+        self.all_of(self.others(self.joined), self.sc, self.rc).wait_recv()
         self.joined_b[...] = self.joined[...].astype(BF)
         self.copy_d(0).start()
         self.copy_d(1).start()
@@ -141,8 +147,8 @@
     def settle(self):
         for r in (1, 2, 3):
             self.copy_a(r).wait_send()
-        loop(self.n_dp, lambda r: self.copy_b(r).wait_send(), first=1)
-        loop(self.n_dp, lambda r: self.copy_c(r).wait_send(), first=1)
+        self.all_of(self.pieces, self.sb, self.rb).wait_send()
+        self.all_of(self.others(self.joined), self.sc, self.rc).wait_send()
         for k in range(3):
             self.copy_d(k).wait_send()
 
@@ -152,10 +158,11 @@
         return [
             VM((1024, 128), BF), VM((3, 256, 128), BF), VM((256, 128), F32), VM((n_dp - 1, size, 128), F32),
             VM((size, 128), F32), VM((256, 128), F32), VM((256, 128), BF), VM((1024, 128), BF),
-        ] + [DMA((3,))] * 2 + [DMA((n_dp - 1,))] * 4 + [DMA((3,))] * 2
+        ] + [DMA((3,))] * 2 + [DMA] * 4 + [DMA((3,))] * 2
 
 
 N_IN, N_OUT, N_SUM = 15, 12, 16
+GROUP = 4
 
 
 def kernel(n_dp, factor, *refs):
@@ -178,8 +185,8 @@
     barrier = pltpu.get_barrier_semaphore()
     for r in range(1, 4):
         pl.semaphore_signal(barrier, inc=1, device_id={"dap": lax.rem(a + r, 4)}, device_id_type=MESH)
-    loop(n_dp, lambda r: pl.semaphore_signal(
-        barrier, inc=1, device_id={"dp": lax.rem(p + r, n_dp)}, device_id_type=MESH), first=1)
+    for r in range(1, n_dp):
+        pl.semaphore_signal(barrier, inc=1, device_id={"dp": lax.rem(p + r, n_dp)}, device_id_type=MESH)
 
     rows_i = lax.broadcasted_iota(jnp.int32, (128, 128), 0)
     unit = (rows_i == lax.broadcasted_iota(jnp.int32, (128, 128), 1)).astype(F32).astype(BF)
@@ -219,13 +226,14 @@
 
 
     def edge(kind, c):
-        spot = right.at[cross if kind == 2 else a, at(c, 8)]
+        block = right.at[cross if kind == 2 else a]
+        spot = block.at[8 * c : 8 * c + 8] if c < 2 else block.at[16:32, 64 * (c - 2) : 64 * (c - 1), :]
         return pltpu.make_async_remote_copy(
             src_ref=spot, dst_ref=spot, send_sem=sem_es.at[kind, c], recv_sem=sem_er.at[kind, c],
             device_id={"dap": cross if kind == 1 else partner}, device_id_type=MESH)
 
-    def project(c, t):
-        i = c * 8 + 2 * t
+    def project(t):
+        i = 2 * t
         hat, _ = norm_cols(flipped(slab, i))
         n = (hat * twice(g1[...])).astype(BF)
         q = mm(w1t[...], n)
@@ -244,39 +252,47 @@
             pieces[i + r, 256:384] = q[384:512, lanes(r)]
             pieces[i + r, 384:512] = sb[:, lanes(r)]
 
-    def first(c):
-        loop(4, lambda t: project(c, t), 2)
-        pl.when(c == 0)(lambda: pl.semaphore_wait(barrier, 3 + n_dp - 1))
+    loop(4, project, 2)
+    pl.semaphore_wait(barrier, 3 + n_dp - 1)
+    for c, (low_t, high_t) in enumerate(((0, 0), (4, 8), (8, 16), (0, 0))):
+        if high_t > low_t:
+            loop(high_t, project, 2, first=low_t)
         edge(1, c).start()
         edge(0, c).start()
 
-    loop(4, first)
-
-    def unpack(block, base):
-        loop(32, lambda j: right_f.__setitem__((at(base + j, 128), slice(None)), right[block, j].astype(F32)), 2)
-
-    def multiply(half):
+    def unpack(block, base, rows=(0, 32), chans=(0, 128)):
+        span = slice(*chans)
+
+        def one(j):
+            start = pl.multiple_of((base + j) * 128 + chans[0], 64)
+            right_f[pl.ds(start, chans[1] - chans[0]), :] = right[block, j, span].astype(F32)
+
+        loop(rows[1], one, 4, first=rows[0])
+
+    def multiply(half, chans=(0, 128)):
         def one(ch):
             lft = left_f[pl.ds(ch, 32, stride=128), :].astype(BF)
             rgt = right_f[pl.ds(64 * 128 * half + ch, 64, stride=128), :].astype(BF)
             prod[at(ch, 32), 64 * half : 64 * half + 64] = nt(lft, rgt)
-        loop(128, one, 16)
-
-    loop(4, lambda c: edge(0, c).wait_recv())
+        loop(chans[1], one, 16, first=chans[0])
+
+    for c in range(4):
+        edge(0, c).wait_recv()
     low = 2 * chip
     unpack(low, 0)
     unpack(low + 1, 32)
     multiply(0)
 
-    def relay(c):
+    beside = cross + 1 - 2 * core
+    for c in range(4):
+        rows, chans = ((8 * c, 8 * c + 8), (0, 128)) if c < 2 else ((16, 32), (64 * (c - 2), 64 * (c - 1)))
         edge(1, c).wait_recv()
         edge(2, c).start()
-
-    loop(4, relay)
-    loop(4, lambda c: edge(2, c).wait_recv())
-    unpack(2 - low, 64)
-    unpack(3 - low, 96)
-    multiply(1)
+        unpack(cross, 64 + 32 * core, rows, chans)
+        edge(2, c).wait_recv()
+        unpack(beside, 96 - 32 * core, rows, chans)
+        if c >= 2:
+            multiply(1, chans)
 
     def second(t):
         i = 2 * t
@@ -319,11 +335,11 @@
         bt[:, lanes(h)] += flip(bias[h])
 
 
-    def spread(x):
+    def spread(x, h0):
         zero = jnp.zeros((32, 128), x.dtype)
         cols = [
             jnp.concatenate([x[32 * h : 32 * h + 32] if g == h else zero for g in range(4)], axis=0)
-            for h in range(4)
+            for h in range(h0, h0 + GROUP)
         ]
         return jnp.concatenate(cols, axis=1)
 
@@ -343,30 +359,35 @@
         picked = lax.broadcasted_iota(jnp.int32, (32, 256), 0) == (
             i + lax.broadcasted_iota(jnp.int32, (32, 256), 1) // 128)
         alive = mm(live_t[...], picked.astype(F32).astype(BF))
-        parts, atts = [], []
-        for r in range(2):
-            q, k, v = (qkv[128 * x : 128 * x + 128, lanes(r)] for x in range(3))
-            kv = flip(qkv[128:384, lanes(r)]).astype(BF)
-            q4 = spread(q)
-            e = jnp.exp(mm(kv[:, :128], q4) * scale + bt[...])
-            e = e * jnp.concatenate([alive[:, lanes(r)]] * 4, axis=1)
-            s = jnp.sum(e, axis=0, keepdims=True)
-            w = e * (1.0 / jnp.maximum(s, 1.0))
-            ab = w.astype(BF)
-            atts.append(jnp.concatenate([mm(v[32 * h : 32 * h + 32], ab[:, lanes(h)]) for h in range(4)], axis=0))
-            do4 = spread(d_att[:, lanes(r)].astype(BF))
-            da = mm(kv[:, 128:], do4).astype(BF).astype(F32)
-            u = da * w
-            total = jnp.sum(u, axis=0, keepdims=True)
-            total = jnp.where(s > 1.0, total, jnp.where(s == 1.0, 0.5 * total, 0.0))
-            ds = u - w * total
-            d_bias[...] += ds
-            dsb = ds.astype(BF)
-            dv = nt(do4, ab)
-            dk = nt(q4, dsb) * scale
-            dq = jnp.concatenate(
-                [mm(k[32 * h : 32 * h + 32], dsb[:, lanes(h)]) for h in range(4)], axis=0) * scale
-            parts.append(jnp.concatenate([dq, dk, dv], axis=0).astype(BF))
+        both = range(2)
+        qs, ks, vs = ([qkv[128 * x : 128 * x + 128, lanes(r)] for r in both] for x in range(3))
+        kvs = [flip(qkv[128:384, lanes(r)]).astype(BF) for r in both]
+        dos = [d_att[:, lanes(r)].astype(BF) for r in both]
+        scores = [mm(kvs[r][:, :128], spread(qs[r], 0)) for r in both]
+        das = [mm(kvs[r][:, 128:], spread(dos[r], 0)).astype(BF) for r in both]
+        exps = [
+            jnp.exp(scores[r] * scale + bt[...]) * jnp.concatenate([alive[:, lanes(r)]] * 4, axis=1) for r in both
+        ]
+        sums = [jnp.sum(e, axis=0, keepdims=True) for e in exps]
+        ws = [e * (1.0 / jnp.maximum(s, 1.0)) for e, s in zip(exps, sums)]
+        abs_ = [w.astype(BF) for w in ws]
+        us = [da.astype(F32) * w for da, w in zip(das, ws)]
+        totals = [jnp.sum(u, axis=0, keepdims=True) for u in us]
+        totals = [
+            jnp.where(s > 1.0, x, jnp.where(s == 1.0, 0.5 * x, 0.0)) for s, x in zip(sums, totals)
+        ]
+        dss = [u - w * x for u, w, x in zip(us, ws, totals)]
+        d_bias[...] += dss[0] + dss[1]
+        dsbs = [ds.astype(BF) for ds in dss]
+
+        def heads_of(fn):
+            return jnp.concatenate([fn(slice(32 * h, 32 * h + 32), lanes(h)) for h in range(4)], axis=0)
+
+        atts = [heads_of(lambda h, l: mm(vs[r][h], abs_[r][:, l])) for r in both]
+        dvs = [heads_of(lambda h, l: nt(dos[r][h], abs_[r][:, l])) for r in both]
+        dks = [heads_of(lambda h, l: nt(qs[r][h], dsbs[r][:, l])) * scale for r in both]
+        dqs = [heads_of(lambda h, l: mm(ks[r][h], dsbs[r][:, l])) * scale for r in both]
+        parts = [jnp.concatenate([dqs[r], dks[r], dvs[r]], axis=0).astype(BF) for r in both]
         att = jnp.concatenate(atts, axis=1)
         d_open = (d_gated * att * gate * (1.0 - gate)).astype(BF)
         dp = jnp.concatenate([jnp.concatenate(parts, axis=1), d_open], axis=0)
@@ -566,7 +587,8 @@
         share_bias(r).wait_send()
         share_grad(r).wait_send()
     for kind in range(3):
-        loop(4, lambda c: edge(kind, c).wait_send())
+        for c in range(4):
+            edge(kind, c).wait_send()
         loop(4, lambda q: move(kind, q).wait_send())
     late.start_d()
     late.finish()

time: 163 us -> 152 us (0.933)
  Pallas kernels: 162 us -> 151 us
    pallas_call x1, Pallas kernels: 159 us -> 148 us  [per_device(): pl.pallas_call(partial(kernel, n_dp, factor), out_shape=[jax.ShapeDtypeSt...]
where the time goes in v3:
time: 152 us
  Pallas kernels  151 us (99%)
    pallas_call x1, Pallas kernels, per_device(): pl.pallas_call(partial(kernel, n_dp, factor), out_shape=[jax.ShapeDtypeSt...  148 us

profile of v3, /device:TPU:1, one launch (start us, length us, event | category | flops | bytes accessed | tf_op | source)
XLA Modules:
  0.0 152.1 jit_solution(16424242839520928744)
XLA Ops:
  0.7 148.4 %pairformer.1 = (bf16[32,128,128]{2,1,0:T(8,128)(2,1)}, bf16[32,128,128]{2,1,0:T(8,128)(2,1)}, f32[1,128]{1,0:T(1,128)}, f32[128,512]{1,0:T(8,128)}, f32[128,128...) custom-call(bf16[32,128,128]{2,1,0:T(8,128)(2,1)} %bitcast.13, ...), custom_call_target="tpu_custom_call" | custom-call | tf_op jit(solution)/shard_map/pairformer/pallas_call | solution.py:644
  149.1 2.8 %hand_over.1 = (bf16[32,128,128]{2,1,0:T(8,128)(2,1)}, bf16[32,128,128]{2,1,0:T(8,128)(2,1)}, f32[1,128]{1,0:T(1,128)}, f32[128,512]{1,0:T(8,128)}, f32[128,128]...) custom-call(bf16[32,128,128]{2,1,0:T(8,128)(2,1)} %get-tuple-element, ...), custom_call_target="tpu_custom_call" | custom-call | tf_op jit(solution)/shard_map/hand_over/pallas_call | solution.py:654

commit v4 on v3

--- a/solution.py
+++ b/solution.py
@@ -162,7 +162,7 @@
 
 
 N_IN, N_OUT, N_SUM = 15, 12, 16
-GROUP = 4
+STRIP, SPLIT = 16, 8
 
 
 def kernel(n_dp, factor, *refs):
@@ -179,7 +179,7 @@
      mid, dn3, prod, right, left_f, right_f, gates, pieces, normed, bias_f, bias_b, bias,
      d_bias, d_wa, d_wo, d_wout, d_wb, d_w1, gain_sum,
      db_n, db_in, db_f, d_prod, d_mid, d_gate, work, far, far_in, sent, cross_in, near, near_in,
-     sem_es, sem_er, sem_is, sem_ir, sem_bs, sem_br, sem_s, sem_r) = rest[2 * N_SUM :]
+     slab_t, cot_t, d_gated_t, scales, sem_es, sem_er, sem_is, sem_ir, sem_bs, sem_br, sem_s, sem_r) = rest[2 * N_SUM :]
     part = gates
 
     barrier = pltpu.get_barrier_semaphore()
@@ -234,23 +234,28 @@
 
     def project(t):
         i = 2 * t
-        hat, _ = norm_cols(flipped(slab, i))
+        x = flipped(slab, i)
+        hat, _ = norm_cols(x)
         n = (hat * twice(g1[...])).astype(BF)
         q = mm(w1t[...], n)
         alive = alive_of(i)
         sa, sb = jax.nn.sigmoid(q[128:256]), jax.nn.sigmoid(q[512:])
-        lft = (sa * q[:128] * alive).astype(BF).astype(F32)
-        rgt = (sb * q[384:512] * alive).astype(BF)
+        fa, fb = sa * alive, sb * alive
+        lft, rgt = fa * q[:128], fb * q[384:512]
+        ga, gb = lft * (1.0 - sa), rgt * (1.0 - sb)
+        lft, rgt = lft.astype(BF).astype(F32), rgt.astype(BF)
+        x = x.astype(BF)
         gate = jax.nn.sigmoid(q[256:384])
         for r in range(2):
             normed[i + r] = n[:, lanes(r)]
+            slab_t[i + r] = x[:, lanes(r)]
             left_f[at(i + r, 128), :] = lft[:, lanes(r)]
             right[a, i + r] = rgt[:, lanes(r)]
             gates[i + r] = gate[:, lanes(r)]
-            pieces[i + r, 0:128] = q[:128, lanes(r)]
-            pieces[i + r, 128:256] = sa[:, lanes(r)]
-            pieces[i + r, 256:384] = q[384:512, lanes(r)]
-            pieces[i + r, 384:512] = sb[:, lanes(r)]
+            pieces[i + r, 0:128] = fa[:, lanes(r)]
+            pieces[i + r, 128:256] = ga[:, lanes(r)]
+            pieces[i + r, 256:384] = fb[:, lanes(r)]
+            pieces[i + r, 384:512] = gb[:, lanes(r)]
 
     loop(4, project, 2)
     pl.semaphore_wait(barrier, 3 + n_dp - 1)
@@ -282,6 +287,16 @@
     unpack(low, 0)
     unpack(low + 1, 32)
     multiply(0)
+
+    def prepare(t):
+        i = 2 * t
+        ct = flipped(cot, i).astype(BF)
+        dg = mm(att_out[...], ct).astype(BF)
+        for r in range(2):
+            cot_t[i + r] = ct[:, lanes(r)]
+            d_gated_t[i + r] = dg[:, lanes(r)]
+
+    loop(16, prepare, 4)
 
     beside = cross + 1 - 2 * core
     for c in range(4):
@@ -304,7 +319,7 @@
             xs.append(x)
         hat, _ = norm_cols(jnp.concatenate(xs, axis=1))
         n = (hat * twice(g2[...])).astype(BF)
-        middle = (flipped(slab, i) + pair(gates, i) * mm(woutt[...], n)).astype(BF)
+        middle = (pair(slab_t, i).astype(F32) + pair(gates, i) * mm(woutt[...], n)).astype(BF)
         hat, _ = norm_cols(middle.astype(F32))
         n = (hat * twice(g3[...])).astype(BF)
         heads = mm(wbt[...], n)
@@ -335,11 +350,11 @@
         bt[:, lanes(h)] += flip(bias[h])
 
 
-    def spread(x, h0):
+    def spread(x):
         zero = jnp.zeros((32, 128), x.dtype)
         cols = [
             jnp.concatenate([x[32 * h : 32 * h + 32] if g == h else zero for g in range(4)], axis=0)
-            for h in range(h0, h0 + GROUP)
+            for h in range(4)
         ]
         return jnp.concatenate(cols, axis=1)
 
@@ -353,8 +368,8 @@
         q3 = mm(wat[...], n)
         qkv = q3[:384].astype(BF)
         gate = jax.nn.sigmoid(q3[384:])
-        ct = flipped(cot, i).astype(BF)
-        d_gated = mm(att_out[...], ct).astype(BF).astype(F32)
+        ct = pair(cot_t, i)
+        d_gated = pair(d_gated_t, i).astype(F32)
         d_att = d_gated * gate
         picked = lax.broadcasted_iota(jnp.int32, (32, 256), 0) == (
             i + lax.broadcasted_iota(jnp.int32, (32, 256), 1) // 128)
@@ -363,8 +378,8 @@
         qs, ks, vs = ([qkv[128 * x : 128 * x + 128, lanes(r)] for r in both] for x in range(3))
         kvs = [flip(qkv[128:384, lanes(r)]).astype(BF) for r in both]
         dos = [d_att[:, lanes(r)].astype(BF) for r in both]
-        scores = [mm(kvs[r][:, :128], spread(qs[r], 0)) for r in both]
-        das = [mm(kvs[r][:, 128:], spread(dos[r], 0)).astype(BF) for r in both]
+        scores = [mm(kvs[r][:, :128], spread(qs[r])) for r in both]
+        das = [mm(kvs[r][:, 128:], spread(dos[r])).astype(BF) for r in both]
         exps = [
             jnp.exp(scores[r] * scale + bt[...]) * jnp.concatenate([alive[:, lanes(r)]] * 4, axis=1) for r in both
         ]
@@ -444,7 +459,7 @@
         dn = pair(dn3, i).astype(F32) + mm(wb[...], db)
         d_wb[...] += nt(db, n3)
         gain_sum[2] += fold(dn * hat3)
-        dm = flipped(cot, i).astype(BF) + norm_back(dn * gain3, hat3, scale3).astype(BF)
+        dm = pair(cot_t, i) + norm_back(dn * gain3, hat3, scale3).astype(BF)
         dmf = dm.astype(F32)
         x = jnp.concatenate([prod[pl.ds(i, 128, stride=32), :], prod[pl.ds(i + 1, 128, stride=32), :]], axis=1)
         hat2, scale2 = norm_cols(x)
@@ -466,7 +481,7 @@
     early.start_b()
 
     def chunk(ref, q):
-        return ref.at[:, at(q, 32), :]
+        return ref.at[:, at(q, STRIP), :]
 
     def move(kind, q):
         src, dst, peer = (
@@ -478,25 +493,25 @@
 
     def right_grads(half, q, store):
         def one(c):
-            ch = 32 * q + c
+            ch = STRIP * q + c
             dp = d_prod[at(ch, 32), 64 * half : 64 * half + 64].astype(BF)
-            work[pl.ds(c, 64, stride=32), :] = tn(dp, left_f[pl.ds(ch, 32, stride=128), :].astype(BF))
-
-        loop(32, one, 16)
+            work[pl.ds(c, 64, stride=STRIP), :] = tn(dp, left_f[pl.ds(ch, 32, stride=128), :].astype(BF))
+
+        loop(STRIP, one, 16)
 
         def pack(j):
-            store[j // 32, lax.rem(j, 32), at(q, 32), :] = work[at(j, 32), :].astype(BF)
-
-        loop(64, pack, 4)
+            store[j // 32, lax.rem(j, 32), at(q, STRIP), :] = work[at(j, STRIP), :].astype(BF)
+
+        loop(64, pack, 8)
 
     def add_on(q):
         move(0, q).wait_recv()
 
         def one(j):
-            spot = at(q, 32)
+            spot = at(q, STRIP)
             sent[j, spot, :] = (far[core, j, spot, :].astype(F32) + far_in[j, spot, :].astype(F32)).astype(BF)
 
-        loop(32, one, 4)
+        loop(32, one, 8)
         move(1, q).start()
 
     def out_far(q):
@@ -504,14 +519,14 @@
         move(0, q).start()
         pl.when(q > 0)(lambda: add_on(q - 1))
 
-    loop(4, out_far)
+    loop(SPLIT, out_far)
 
     def out_near(q):
         right_grads(0, q, near)
         move(2, q).start()
-        pl.when(q == 0)(lambda: add_on(3))
-
-    loop(4, out_near)
+        pl.when(q == 0)(lambda: add_on(SPLIT - 1))
+
+    loop(SPLIT, out_near)
     early.start_c()
 
     def left_grad(ch):
@@ -520,10 +535,6 @@
 
     loop(128, left_grad, 16)
 
-    def sides(grad_in, x, s, alive):
-        g = grad_in * alive * s
-        return g, g * x * (1.0 - s)
-
     def stored(i, k):
         rows = slice(128 * k, 128 * k + 128)
         return jnp.concatenate([pieces[i, rows], pieces[i + 1, rows]], axis=1)
@@ -531,8 +542,8 @@
     def left_part(t):
         i = 2 * t
         dl = jnp.concatenate([left_f[at(i, 128), :], left_f[at(i + 1, 128), :]], axis=1).astype(BF).astype(F32)
-        dpa, dga = sides(dl, stored(i, 0), stored(i, 1), alive_of(i))
-        dp = jnp.concatenate([dpa.astype(BF), dga.astype(BF), pair(d_gate, i)], axis=0)
+        dp = jnp.concatenate(
+            [(dl * stored(i, 0)).astype(BF), (dl * stored(i, 1)).astype(BF), pair(d_gate, i)], axis=0)
         d_w1[0:384, :] += nt(dp, pair(normed, i))
         dn = mm(w1[:, 0:384], dp)
         part[i] = dn[:, :128]
@@ -540,23 +551,32 @@
 
     loop(16, left_part, 4)
 
-    loop(4, lambda q: move(2, q).wait_recv())
-    loop(4, lambda q: move(1, q).wait_recv())
+    loop(SPLIT, lambda q: move(2, q).wait_recv())
+
+    def settle_near(t):
+        i = 2 * t
+        hat, scale_1 = norm_cols(pair(slab_t, i).astype(F32))
+        for r in range(2):
+            right_f[at(i + r, 128), :] = near[core, i + r].astype(F32) + near_in[i + r].astype(F32)
+            right_f[at(32 + i + r, 128), :] = hat[:, lanes(r)]
+            scales[pl.ds(i + r, 1), :] = scale_1[:, lanes(r)]
+
+    loop(16, settle_near, 2)
+    loop(SPLIT, lambda q: move(1, q).wait_recv())
     early.start_d()
 
     def right_part(t):
         i = 2 * t
 
-        def summed(j):
-            x = near[core, j].astype(F32) + near_in[j].astype(F32) + cross_in[j].astype(F32)
-            return x.astype(BF).astype(F32)
-
-        dr = jnp.concatenate([summed(i), summed(i + 1)], axis=1)
-        dpb, dgb = sides(dr, stored(i, 2), stored(i, 3), alive_of(i))
-        dp = jnp.concatenate([dpb.astype(BF), dgb.astype(BF)], axis=0)
+        def held(j):
+            return jnp.concatenate([right_f[at(j, 128), :], right_f[at(j + 1, 128), :]], axis=1)
+
+        dr = (held(i) + pair(cross_in, i).astype(F32)).astype(BF).astype(F32)
+        dp = jnp.concatenate([(dr * stored(i, 2)).astype(BF), (dr * stored(i, 3)).astype(BF)], axis=0)
         d_w1[384:640, :] += nt(dp, pair(normed, i))
         dn = (pair(part, i) + mm(w1[:, 384:640], dp)).astype(BF).astype(F32)
-        hat, spread_1 = norm_cols(flipped(slab, i))
+        hat = held(32 + i)
+        spread_1 = jnp.concatenate([scales[pl.ds(i, 1), :], scales[pl.ds(i + 1, 1), :]], axis=1)
         gain_sum[0] += fold(dn * hat)
         dx = norm_back(dn * twice(g1[...]), hat, spread_1).astype(BF)
         res = pair(d_mid, i) + dx
@@ -589,7 +609,7 @@
     for kind in range(3):
         for c in range(4):
             edge(kind, c).wait_send()
-        loop(4, lambda q: move(kind, q).wait_send())
+        loop(SPLIT, lambda q: move(kind, q).wait_send())
     late.start_d()
     late.finish()
     for b, source in enumerate((0, 1, 3, 4)):
@@ -637,9 +657,10 @@
         VM((128, 512), F32), VM((512, 128), F32), VM((128, 128), F32), VM((128, 128), F32), VM((16, 128), F32),
         VM((640, 128), F32), VM((3, 128, 128), F32),
         VM((4, 128, 128), BF), VM((3, 4, 32, 128), BF), VM((4, 32, 128), F32), VM((4096, 128), F32),
-        VM(block, BF), VM(block, BF), VM((2048, 128), F32),
+        VM(block, BF), VM(block, BF), VM((64 * STRIP, 128), F32),
         VM((2,) + block, BF), VM(block, BF), VM(block, BF), VM(block, BF), VM((2,) + block, BF), VM(block, BF),
-        DMA((3, 4)), DMA((3, 4)), DMA((3,)), DMA((3,)), DMA((3,)), DMA((3,)), DMA((3, 4)), DMA((3, 4)),
+        VM(block, BF), VM(block, BF), VM(block, BF), VM((32, 128), F32),
+        DMA((3, 4)), DMA((3, 4)), DMA((3,)), DMA((3,)), DMA((3,)), DMA((3,)), DMA((3, SPLIT)), DMA((3, SPLIT)),
     ]
     results = pl.pallas_call(
         partial(kernel, n_dp, factor),

time: 152 us -> 147 us (0.967)
  Pallas kernels: 151 us -> 146 us
    pallas_call x1, Pallas kernels: 148 us -> 143 us  [per_device(): pl.pallas_call(partial(kernel, n_dp, factor), out_shape=[jax.ShapeDtypeSt...]
where the time goes in v4:
time: 147 us
  Pallas kernels  146 us (99%)
    pallas_call x1, Pallas kernels, per_device(): pl.pallas_call(partial(kernel, n_dp, factor), out_shape=[jax.ShapeDtypeSt...  143 us

profile of v4, /device:TPU:1, one launch (start us, length us, event | category | flops | bytes accessed | tf_op | source)
XLA Modules:
  0.0 146.7 jit_solution(8780402297042680441)
XLA Ops:
  0.7 143.2 %pairformer.1 = (bf16[32,128,128]{2,1,0:T(8,128)(2,1)}, bf16[32,128,128]{2,1,0:T(8,128)(2,1)}, f32[1,128]{1,0:T(1,128)}, f32[128,512]{1,0:T(8,128)}, f32[128,128...) custom-call(bf16[32,128,128]{2,1,0:T(8,128)(2,1)} %bitcast.13, ...), custom_call_target="tpu_custom_call" | custom-call | tf_op jit(solution)/shard_map/pairformer/pallas_call | solution.py:665
  143.8 2.8 %hand_over.1 = (bf16[32,128,128]{2,1,0:T(8,128)(2,1)}, bf16[32,128,128]{2,1,0:T(8,128)(2,1)}, f32[1,128]{1,0:T(1,128)}, f32[128,512]{1,0:T(8,128)}, f32[128,128]...) custom-call(bf16[32,128,128]{2,1,0:T(8,128)(2,1)} %get-tuple-element, ...), custom_call_target="tpu_custom_call" | custom-call | tf_op jit(solution)/shard_map/hand_over/pallas_call | solution.py:675

commit v5 on v4

--- a/solution.py
+++ b/solution.py
@@ -179,7 +179,7 @@
      mid, dn3, prod, right, left_f, right_f, gates, pieces, normed, bias_f, bias_b, bias,
      d_bias, d_wa, d_wo, d_wout, d_wb, d_w1, gain_sum,
      db_n, db_in, db_f, d_prod, d_mid, d_gate, work, far, far_in, sent, cross_in, near, near_in,
-     slab_t, cot_t, d_gated_t, scales, sem_es, sem_er, sem_is, sem_ir, sem_bs, sem_br, sem_s, sem_r) = rest[2 * N_SUM :]
+     slab_t, cot_t, d_gated_t, scales, zs, sem_es, sem_er, sem_is, sem_ir, sem_bs, sem_br, sem_s, sem_r) = rest[2 * N_SUM :]
     part = gates
 
     barrier = pltpu.get_barrier_semaphore()
@@ -249,7 +249,7 @@
         for r in range(2):
             normed[i + r] = n[:, lanes(r)]
             slab_t[i + r] = x[:, lanes(r)]
-            left_f[at(i + r, 128), :] = lft[:, lanes(r)]
+            left_f[pl.ds((i + r) * 129, 128), :] = lft[:, lanes(r)]
             right[a, i + r] = rgt[:, lanes(r)]
             gates[i + r] = gate[:, lanes(r)]
             pieces[i + r, 0:128] = fa[:, lanes(r)]
@@ -269,16 +269,16 @@
         span = slice(*chans)
 
         def one(j):
-            start = pl.multiple_of((base + j) * 128 + chans[0], 64)
+            start = (base + j) * 129 + chans[0]
             right_f[pl.ds(start, chans[1] - chans[0]), :] = right[block, j, span].astype(F32)
 
         loop(rows[1], one, 4, first=rows[0])
 
     def multiply(half, chans=(0, 128)):
         def one(ch):
-            lft = left_f[pl.ds(ch, 32, stride=128), :].astype(BF)
-            rgt = right_f[pl.ds(64 * 128 * half + ch, 64, stride=128), :].astype(BF)
-            prod[at(ch, 32), 64 * half : 64 * half + 64] = nt(lft, rgt)
+            lft = left_f[pl.ds(ch, 32, stride=129), :].astype(BF)
+            rgt = right_f[pl.ds(64 * 129 * half + ch, 64, stride=129), :].astype(BF)
+            prod[pl.ds(ch * 33, 32), 64 * half : 64 * half + 64] = nt(lft, rgt)
         loop(chans[1], one, 16, first=chans[0])
 
     for c in range(4):
@@ -313,13 +313,16 @@
         i = 2 * t
         xs = []
         for r in range(2):
-            rows = pl.ds(i + r, 128, stride=32)
-            x = pltpu.roll(prod[rows, :], 64 * chip, axis=1)
-            prod[rows, :] = x
-            xs.append(x)
-        hat, _ = norm_cols(jnp.concatenate(xs, axis=1))
+            rows = pl.ds(i + r, 128, stride=33)
+            xs.append(pltpu.roll(prod[rows, :], 64 * chip, axis=1))
+        hat, scale_2 = norm_cols(jnp.concatenate(xs, axis=1))
         n = (hat * twice(g2[...])).astype(BF)
-        middle = (pair(slab_t, i).astype(F32) + pair(gates, i) * mm(woutt[...], n)).astype(BF)
+        z = mm(woutt[...], n)
+        for r in range(2):
+            prod[pl.ds(i + r, 128, stride=33), :] = hat[:, lanes(r)]
+            scales[pl.ds(32 + i + r, 1), :] = scale_2[:, lanes(r)]
+            zs[i + r] = z[:, lanes(r)]
+        middle = (pair(slab_t, i).astype(F32) + pair(gates, i) * z).astype(BF)
         hat, _ = norm_cols(middle.astype(F32))
         n = (hat * twice(g3[...])).astype(BF)
         heads = mm(wbt[...], n)
@@ -415,7 +418,7 @@
             dn3[i + r] = dn[:, lanes(r)]
             out[i + r] = flip(res[:, lanes(r)]).astype(BF)
 
-    loop(16, attend, 2)
+    loop(16, attend, 4)
 
     for h in range(4):
         db_n[h] = flip(d_bias[:, lanes(h)].astype(BF)).astype(BF)
@@ -461,10 +464,10 @@
         gain_sum[2] += fold(dn * hat3)
         dm = pair(cot_t, i) + norm_back(dn * gain3, hat3, scale3).astype(BF)
         dmf = dm.astype(F32)
-        x = jnp.concatenate([prod[pl.ds(i, 128, stride=32), :], prod[pl.ds(i + 1, 128, stride=32), :]], axis=1)
-        hat2, scale2 = norm_cols(x)
+        hat2 = jnp.concatenate([prod[pl.ds(i, 128, stride=33), :], prod[pl.ds(i + 1, 128, stride=33), :]], axis=1)
+        scale2 = jnp.concatenate([scales[pl.ds(32 + i, 1), :], scales[pl.ds(33 + i, 1), :]], axis=1)
         n2 = (hat2 * gain2).astype(BF)
-        z = mm(woutt[...], n2)
+        z = pair(zs, i)
         gate = pair(gates, i)
         dz = (dmf * gate).astype(BF)
         d_open = (dmf * z * gate * (1.0 - gate)).astype(BF)
@@ -473,12 +476,11 @@
         gain_sum[1] += fold(dn2 * hat2)
         dp = norm_back(dn2 * gain2, hat2, scale2)
         for r in range(2):
-            d_prod[pl.ds(i + r, 128, stride=32), :] = pltpu.roll(dp[:, lanes(r)], 64 * chip, axis=1)
+            d_prod[pl.ds(i + r, 128, stride=33), :] = pltpu.roll(dp[:, lanes(r)], 64 * chip, axis=1)
             d_mid[i + r] = dm[:, lanes(r)]
             d_gate[i + r] = d_open[:, lanes(r)]
 
     loop(16, second_back, 4)
-    early.start_b()
 
     def chunk(ref, q):
         return ref.at[:, at(q, STRIP), :]
@@ -494,13 +496,13 @@
     def right_grads(half, q, store):
         def one(c):
             ch = STRIP * q + c
-            dp = d_prod[at(ch, 32), 64 * half : 64 * half + 64].astype(BF)
-            work[pl.ds(c, 64, stride=STRIP), :] = tn(dp, left_f[pl.ds(ch, 32, stride=128), :].astype(BF))
+            dp = d_prod[pl.ds(ch * 33, 32), 64 * half : 64 * half + 64].astype(BF)
+            work[pl.ds(c, 64, stride=STRIP + 1), :] = tn(dp, left_f[pl.ds(ch, 32, stride=129), :].astype(BF))
 
         loop(STRIP, one, 16)
 
         def pack(j):
-            store[j // 32, lax.rem(j, 32), at(q, STRIP), :] = work[at(j, STRIP), :].astype(BF)
+            store[j // 32, lax.rem(j, 32), at(q, STRIP), :] = work[pl.ds(j * (STRIP + 1), STRIP), :].astype(BF)
 
         loop(64, pack, 8)
 
@@ -520,6 +522,7 @@
         pl.when(q > 0)(lambda: add_on(q - 1))
 
     loop(SPLIT, out_far)
+    early.start_b()
 
     def out_near(q):
         right_grads(0, q, near)
@@ -530,8 +533,8 @@
     early.start_c()
 
     def left_grad(ch):
-        rgt = right_f[pl.ds(ch, 128, stride=128), :].astype(BF)
-        left_f[pl.ds(ch, 32, stride=128), :] = mm(d_prod[at(ch, 32), :].astype(BF), rgt)
+        rgt = right_f[pl.ds(ch, 128, stride=129), :].astype(BF)
+        left_f[pl.ds(ch, 32, stride=129), :] = mm(d_prod[pl.ds(ch * 33, 32), :].astype(BF), rgt)
 
     loop(128, left_grad, 16)
 
@@ -541,7 +544,7 @@
 
     def left_part(t):
         i = 2 * t
-        dl = jnp.concatenate([left_f[at(i, 128), :], left_f[at(i + 1, 128), :]], axis=1).astype(BF).astype(F32)
+        dl = jnp.concatenate([left_f[pl.ds(i * 129, 128), :], left_f[pl.ds(i * 129 + 129, 128), :]], axis=1).astype(BF).astype(F32)
         dp = jnp.concatenate(
             [(dl * stored(i, 0)).astype(BF), (dl * stored(i, 1)).astype(BF), pair(d_gate, i)], axis=0)
         d_w1[0:384, :] += nt(dp, pair(normed, i))
@@ -651,15 +654,15 @@
         VM((128, 128), F32), VM((128, 128), F32), VM((128, 128), F32),
         VM((128, 640), BF), VM((640, 128), BF), VM((512, 128), BF), VM((128, 128), BF), VM((128, 128), BF),
         VM((128, 16), BF), VM((16, 128), BF), VM((16, 128), F32), VM((4, 16, 16), F32), VM((128, 512), F32),
-        VM(block, BF), VM(block, BF), VM((4096, 128), F32), VM((4,) + block, BF), VM((4096, 128), F32),
-        VM((16384, 128), F32), VM(block, F32), VM((32, 512, 128), F32), VM(block, BF),
+        VM(block, BF), VM(block, BF), VM((4224, 128), F32), VM((4,) + block, BF), VM((4128, 128), F32),
+        VM((16512, 128), F32), VM(block, F32), VM((32, 512, 128), F32), VM(block, BF),
         VM((4, 32, 128), F32), VM((4, 32, 128), BF), VM((4, 128, 128), BF),
         VM((128, 512), F32), VM((512, 128), F32), VM((128, 128), F32), VM((128, 128), F32), VM((16, 128), F32),
         VM((640, 128), F32), VM((3, 128, 128), F32),
-        VM((4, 128, 128), BF), VM((3, 4, 32, 128), BF), VM((4, 32, 128), F32), VM((4096, 128), F32),
-        VM(block, BF), VM(block, BF), VM((64 * STRIP, 128), F32),
+        VM((4, 128, 128), BF), VM((3, 4, 32, 128), BF), VM((4, 32, 128), F32), VM((4224, 128), F32),
+        VM(block, BF), VM(block, BF), VM((64 * (STRIP + 1), 128), F32),
         VM((2,) + block, BF), VM(block, BF), VM(block, BF), VM(block, BF), VM((2,) + block, BF), VM(block, BF),
-        VM(block, BF), VM(block, BF), VM(block, BF), VM((32, 128), F32),
+        VM(block, BF), VM(block, BF), VM(block, BF), VM((64, 128), F32), VM(block, F32),
         DMA((3, 4)), DMA((3, 4)), DMA((3,)), DMA((3,)), DMA((3,)), DMA((3,)), DMA((3, SPLIT)), DMA((3, SPLIT)),
     ]
     results = pl.pallas_call(

time: 147 us -> 144 us (0.980)
  Pallas kernels: 146 us -> 144 us
    pallas_call x1, Pallas kernels: 143 us -> 141 us  [per_device(): pl.pallas_call(partial(kernel, n_dp, factor), out_shape=[jax.ShapeDtypeSt...]
where the time goes in v5:
time: 144 us
  Pallas kernels  144 us (100%)
    pallas_call x1, Pallas kernels, per_device(): pl.pallas_call(partial(kernel, n_dp, factor), out_shape=[jax.ShapeDtypeSt...  141 us

profile of v5, /device:TPU:1, one launch (start us, length us, event | category | flops | bytes accessed | tf_op | source)
XLA Modules:
  0.0 144.2 jit_solution(17509876519932641686)
XLA Ops:
  0.7 140.7 %pairformer.1 = (bf16[32,128,128]{2,1,0:T(8,128)(2,1)}, bf16[32,128,128]{2,1,0:T(8,128)(2,1)}, f32[1,128]{1,0:T(1,128)}, f32[128,512]{1,0:T(8,128)}, f32[128,128...) custom-call(bf16[32,128,128]{2,1,0:T(8,128)(2,1)} %bitcast.13, ...), custom_call_target="tpu_custom_call" | custom-call | tf_op jit(solution)/shard_map/pairformer/pallas_call | solution.py:668
  141.4 2.8 %hand_over.1 = (bf16[32,128,128]{2,1,0:T(8,128)(2,1)}, bf16[32,128,128]{2,1,0:T(8,128)(2,1)}, f32[1,128]{1,0:T(1,128)}, f32[128,512]{1,0:T(8,128)}, f32[128,128]...) custom-call(bf16[32,128,128]{2,1,0:T(8,128)(2,1)} %get-tuple-element, ...), custom_call_target="tpu_custom_call" | custom-call | tf_op jit(solution)/shard_map/hand_over/pallas_call | solution.py:678

commit v6 on v5

--- a/solution.py
+++ b/solution.py
@@ -85,9 +85,29 @@
         return pltpu.make_async_remote_copy(
             src_ref=src, dst_ref=dst, send_sem=s, recv_sem=r, device_id=peer, device_id_type=MESH)
 
-    def copy_a(self, r):
+    def copy_a(self, r, k):
         peer = lax.rem(self.a + r, 4)
-        return self.remote(self.g.at[at(peer, 256)], self.part.at[r - 1], self.sa.at[r - 1], self.ra.at[r - 1], dap=peer)
+        start, size = ((0, CUT), (CUT, 256 - CUT))[k]
+        src = self.g.at[pl.ds(pl.multiple_of(peer * 256 + start, 16), size)]
+        return self.remote(
+            src, self.part.at[r - 1, start : start + size], self.sa.at[k, r - 1], self.ra.at[k, r - 1], dap=peer)
+
+    def rows_of(self, k, first, size):
+        span = (CUT, 256 - CUT)[k]
+        while size > 0:
+            count = min(size, span - first % span)
+            row = 256 * (first // span) + CUT * k + first % span
+            yield slice(row, row + count), count
+            first, size = first + count, size - count
+
+    def put(self, k, first, block):
+        done = 0
+        for rows, count in self.rows_of(k, first, block.shape[0]):
+            self.g[rows, :] = block[done : done + count].astype(BF)
+            done += count
+
+    def get(self, k, first, size):
+        return jnp.concatenate([self.full[rows, :] for rows, _ in self.rows_of(k, first, size)], axis=0)
 
     def copy_b(self, r):
         peer = lax.rem(self.p + r, self.n_dp)
@@ -110,14 +130,15 @@
         return self.remote(
             src, self.full.at[there], self.sd.at[k], self.rd.at[k], dap=self.cross if k == 0 else self.partner)
 
-    def start_a(self):
+    def start_a(self, k):
         for r in (2, 1, 3):
-            self.copy_a(r).start()
+            self.copy_a(r, k).start()
 
     def start_b(self):
         total = self.g[at(self.a, 256), :].astype(F32)
         for r in (1, 2, 3):
-            self.copy_a(r).wait_recv()
+            for k in range(2):
+                self.copy_a(r, k).wait_recv()
             total = total + self.part[r - 1].astype(F32)
         self.quarter[...] = total
         for r in range(1, self.n_dp):
@@ -146,7 +167,8 @@
 
     def settle(self):
         for r in (1, 2, 3):
-            self.copy_a(r).wait_send()
+            for k in range(2):
+                self.copy_a(r, k).wait_send()
         self.all_of(self.pieces, self.sb, self.rb).wait_send()
         self.all_of(self.others(self.joined), self.sc, self.rc).wait_send()
         for k in range(3):
@@ -158,11 +180,11 @@
         return [
             VM((1024, 128), BF), VM((3, 256, 128), BF), VM((256, 128), F32), VM((n_dp - 1, size, 128), F32),
             VM((size, 128), F32), VM((256, 128), F32), VM((256, 128), BF), VM((1024, 128), BF),
-        ] + [DMA((3,))] * 2 + [DMA] * 4 + [DMA((3,))] * 2
+        ] + [DMA((2, 3))] * 2 + [DMA] * 4 + [DMA((3,))] * 2
 
 
 N_IN, N_OUT, N_SUM = 15, 12, 16
-STRIP, SPLIT = 16, 8
+STRIP, SPLIT, CUT = 16, 8, 176
 
 
 def kernel(n_dp, factor, *refs):
@@ -437,7 +459,8 @@
     for h in range(4):
         near_types = mm(hot[...], d_bias[:, lanes(h)])
         early.g[640 + 16 * h : 656 + 16 * h, 0:16] = nt(hot[...], near_types).astype(BF)
-    early.start_a()
+    early.start_a(0)
+    early.start_a(1)
 
     for r in (1, 2, 3):
         share_grad(r).wait_recv()
@@ -565,8 +588,20 @@
             scales[pl.ds(i + r, 1), :] = scale_1[:, lanes(r)]
 
     loop(16, settle_near, 2)
+    ones = jnp.ones((16, 128), F32)
+
+    def put_gain(k, first, which):
+        late.put(k, first, nt(ones, gain_sum[which], EXACT))
+
+    late.put(0, 0, d_w1[0:384, :])
+    late.put(0, 384, d_wout[...])
+    late.put(0, 512, d_wb[...])
+    put_gain(0, 528, 1)
+    put_gain(0, 544, 2)
+    late.put(0, 560, jnp.zeros((144, 128), F32))
     loop(SPLIT, lambda q: move(1, q).wait_recv())
     early.start_d()
+    late.start_a(0)
 
     def right_part(t):
         i = 2 * t
@@ -589,14 +624,10 @@
     loop(16, right_part, 4)
 
 
-    late.g[0:640, :] = d_w1[...].astype(BF)
-    late.g[640:768, :] = d_wout[...].astype(BF)
-    late.g[768:784, :] = d_wb[...].astype(BF)
-    late.g[784:, :] = jnp.zeros((240, 128), BF)
-    ones = jnp.ones((16, 128), F32)
-    for k in range(3):
-        late.g[784 + 16 * k : 800 + 16 * k, :] = nt(ones, gain_sum[k], EXACT).astype(BF)
-    late.start_a()
+    late.put(1, 0, d_w1[384:640, :])
+    put_gain(1, 256, 0)
+    late.put(1, 272, jnp.zeros((48, 128), F32))
+    late.start_a(1)
     early.finish()
     for b in range(4):
         o_att_in[:, lanes(b)] = flip(early.full[128 * b : 128 * b + 128, :])
@@ -615,13 +646,14 @@
         loop(SPLIT, lambda q: move(kind, q).wait_send())
     late.start_d()
     late.finish()
-    for b, source in enumerate((0, 1, 3, 4)):
-        o_tri_in[:, lanes(b)] = flip(late.full[128 * source : 128 * source + 128, :])
-    o_tri_gate[...] = flip(late.full[256:384, :])
-    o_tri_out[...] = late.full[640:768, :].astype(F32)
-    o_att_bias[...] = late.full[768:784, :].astype(F32)[0:4, :]
-    for k, ref in enumerate((o_gain1, o_gain2, o_gain3)):
-        ref[...] = late.full[784 + 16 * k : 800 + 16 * k, :].astype(F32)[0:1, :]
+    for b in range(2):
+        o_tri_in[:, lanes(b)] = flip(late.get(0, 128 * b, 128))
+        o_tri_in[:, lanes(b + 2)] = flip(late.get(1, 128 * b, 128))
+    o_tri_gate[...] = flip(late.get(0, 256, 128))
+    o_tri_out[...] = late.get(0, 384, 128).astype(F32)
+    o_att_bias[...] = late.get(0, 512, 16).astype(F32)[0:4, :]
+    for ref, k, first in ((o_gain1, 1, 256), (o_gain2, 0, 528), (o_gain3, 0, 544)):
+        ref[...] = late.get(k, first, 16).astype(F32)[0:1, :]
     late.settle()
 
 

time: 144 us -> 144 us (level)
  no operation moved by 1% of the time
where the time goes in v6:
time: 144 us
  Pallas kernels  143 us (99%)
    pallas_call x1, Pallas kernels, per_device(): pl.pallas_call(partial(kernel, n_dp, factor), out_shape=[jax.ShapeDtypeSt...  140 us

profile of v6, /device:TPU:1, one launch (start us, length us, event | category | flops | bytes accessed | tf_op | source)
XLA Modules:
  0.0 143.5 jit_solution(18183970283704951476)
XLA Ops:
  0.7 140.0 %pairformer.1 = (bf16[32,128,128]{2,1,0:T(8,128)(2,1)}, bf16[32,128,128]{2,1,0:T(8,128)(2,1)}, f32[1,128]{1,0:T(1,128)}, f32[128,512]{1,0:T(8,128)}, f32[128,128...) custom-call(bf16[32,128,128]{2,1,0:T(8,128)(2,1)} %bitcast.13, ...), custom_call_target="tpu_custom_call" | custom-call | tf_op jit(solution)/shard_map/pairformer/pallas_call | solution.py:700
  140.7 2.8 %hand_over.1 = (bf16[32,128,128]{2,1,0:T(8,128)(2,1)}, bf16[32,128,128]{2,1,0:T(8,128)(2,1)}, f32[1,128]{1,0:T(1,128)}, f32[128,512]{1,0:T(8,128)}, f32[128,128]...) custom-call(bf16[32,128,128]{2,1,0:T(8,128)(2,1)} %get-tuple-element, ...), custom_call_target="tpu_custom_call" | custom-call | tf_op jit(solution)/shard_map/hand_over/pallas_call | solution.py:710

commit v7 on v6

--- a/solution.py
+++ b/solution.py
@@ -353,7 +353,7 @@
             for h in range(4):
                 bias_f[h, pl.ds(i + r, 1), :] = heads[h : h + 1, lanes(r)]
 
-    loop(16, second, 4)
+    loop(16, second, 8)
     bias_b[...] = bias_f[...].astype(BF)
 
     def share_bias(r):
@@ -440,7 +440,7 @@
             dn3[i + r] = dn[:, lanes(r)]
             out[i + r] = flip(res[:, lanes(r)]).astype(BF)
 
-    loop(16, attend, 4)
+    loop(16, attend, 8)
 
     for h in range(4):
         db_n[h] = flip(d_bias[:, lanes(h)].astype(BF)).astype(BF)
@@ -503,7 +503,7 @@
             d_mid[i + r] = dm[:, lanes(r)]
             d_gate[i + r] = d_open[:, lanes(r)]
 
-    loop(16, second_back, 4)
+    loop(16, second_back, 8)
 
     def chunk(ref, q):
         return ref.at[:, at(q, STRIP), :]
@@ -621,7 +621,7 @@
         grad[i] = flip(res[:, :128]).astype(BF)
         grad[i + 1] = flip(res[:, 128:]).astype(BF)
 
-    loop(16, right_part, 4)
+    loop(16, right_part, 8)
 
 
     late.put(1, 0, d_w1[384:640, :])

time: 144 us -> 143 us (level)
  no operation moved by 1% of the time
where the time goes in v7:
time: 143 us; the launch traced here: 142 us
  Pallas kernels  142 us (99%)
    pallas_call x1, Pallas kernels, per_device(): pl.pallas_call(partial(kernel, n_dp, factor), out_shape=[jax.ShapeDtypeSt...  139 us

profile of v7, /device:TPU:1, one launch (start us, length us, event | category | flops | bytes accessed | tf_op | source)
XLA Modules:
  0.0 142.4 jit_solution(10331520350032316587)
XLA Ops:
  0.7 138.7 %pairformer.1 = (bf16[32,128,128]{2,1,0:T(8,128)(2,1)}, bf16[32,128,128]{2,1,0:T(8,128)(2,1)}, f32[1,128]{1,0:T(1,128)}, f32[128,512]{1,0:T(8,128)}, f32[128,128...) custom-call(bf16[32,128,128]{2,1,0:T(8,128)(2,1)} %bitcast.13, ...), custom_call_target="tpu_custom_call" | custom-call | tf_op jit(solution)/shard_map/pairformer/pallas_call | solution.py:700
  139.4 2.8 %hand_over.1 = (bf16[32,128,128]{2,1,0:T(8,128)(2,1)}, bf16[32,128,128]{2,1,0:T(8,128)(2,1)}, f32[1,128]{1,0:T(1,128)}, f32[128,512]{1,0:T(8,128)}, f32[128,128]...) custom-call(bf16[32,128,128]{2,1,0:T(8,128)(2,1)} %get-tuple-element, ...), custom_call_target="tpu_custom_call" | custom-call | tf_op jit(solution)/shard_map/hand_over/pallas_call | solution.py:710
